TPU v7x, 32 devices: a whole 2x2x4 slice. The times are simulated.
32 devices in a mesh: vis: 8 (over z, x), tile: 4 (over y, core).
Axes of the slice: x: 2, y: 2, z: 4, core: 2. Of those that a mesh axis runs over, the one named last changes fastest.
Arguments:
- vis_data: bfloat16 [32768, 128], P(('vis', 'tile')), may hold values from -0.59765625 to 0.59765625
- u_cell: int32 [16, 32768], P(None, ('vis', 'tile')), may hold values from 0 to 25
- v_cell: int32 [16, 32768], P(None, ('vis', 'tile')), may hold values from 0 to 25
- u_frac: int32 [16, 32768], P(None, ('vis', 'tile')), may hold values from 0 to 15
- v_frac: int32 [16, 32768], P(None, ('vis', 'tile')), may hold values from 0 to 15
- w_plane: int32 [16, 32768], P(None, ('vis', 'tile')), may hold values from 0 to 7
- block_route: int32 [32768, 1], P(('vis', 'tile')), may hold values from 0 to 63; in each aligned block of 1024 rows (0 to 1023, 1024 to 2047, ...) at most 32 rows name the same one
- kernel_taps: float32 [128, 7], replicated, may hold values from 0.1 to 1
- taper_gain: float32 [32, 32], replicated, may hold values from 0.2 to 1
- sub_tile: int32 [256, 1], P(('vis', 'tile')), may hold values from 0 to 7; in each aligned block of 8 rows (0 to 7, 8 to 15, ...) at most 2 rows name the same one
- sub_anchor: int32 [256, 2], P(('vis', 'tile')), may hold values from 0 to 224
Outputs:
- grid_sum: float32 [8, 256, 2048], P('tile', 'vis')
Inputs may be any that keep to these rules, and one draw needn't show every extreme that they name: `block_route`: among the rows of one device at most 32 name one uv-block, and some uv-block is named by exactly 32 of them. `sub_tile`: among the 8 uv-blocks of one device at most 2 map to one grid tile, and some grid tile gets exactly 2 of them.
All inputs are finite; a program needn't handle non-finite values.
Results may differ from a plain program's by a relative error of at most 0.008.
Values may be sent and summed in bfloat16 or wider, within the bound.
A program may use at most 128 MiB of HBM per device.

v0:
```python
import jax
import jax.numpy as jnp
from jax import lax
from jax.sharding import PartitionSpec as P

ROWS_DEV = 1024
BLK_DEV = 8
SUB = 32
CHR = 16
POLC = 8
TAPS = 7
OS = 16
TS = 256
GT_DEV = 2
SCAP = 2


def spread(cell_idx, taps):
    offset = jnp.arange(SUB, dtype=jnp.int32)[None, :] - cell_idx[:, None]
    spread_sum = jnp.zeros((cell_idx.shape[0], SUB), jnp.float32)
    for tap_index in range(TAPS):
        spread_sum = spread_sum + jnp.where(
            offset == tap_index, taps[:, tap_index : tap_index + 1], 0.0
        )
    return spread_sum.astype(jnp.bfloat16)


def lookup(kernel_taps, table_rows):
    picker = (
        table_rows[:, None] == jnp.arange(kernel_taps.shape[0], dtype=jnp.int32)[None, :]
    ).astype(jnp.float32)
    return jnp.dot(picker, kernel_taps, precision=lax.Precision.HIGHEST)


def grid_block(samples, code_rows, kernel_taps, taper_gain):
    taps_u = lookup(kernel_taps, code_rows[2])
    taps_v = lookup(kernel_taps, code_rows[3])
    weight_u = spread(code_rows[0], taps_u)
    weight_v = spread(code_rows[1], taps_v)
    weighted = (
        weight_u.astype(jnp.float32)[:, :, None] * samples.astype(jnp.float32)[:, None, :]
    ).astype(jnp.bfloat16)
    weighted = weighted.reshape(samples.shape[0], SUB * POLC)
    subgrid = lax.dot_general(
        weight_v, weighted, (((0,), (0,)), ((), ())), preferred_element_type=jnp.float32
    )
    return subgrid * jnp.repeat(taper_gain, POLC, axis=1)


def place_tiles(canvas, sub_grids, tile_ids, anchors, first_tile):
    tile_count = canvas.shape[0]

    def add_one(slot_index, canvas):
        target = tile_ids[slot_index] - first_tile
        inside = (target >= 0) & (target < tile_count)
        target = jnp.clip(target, 0, tile_count - 1)
        corner = (
            target,
            anchors[slot_index, 0].astype(jnp.int32),
            (anchors[slot_index, 1] * POLC).astype(jnp.int32),
        )
        window = lax.dynamic_slice(canvas, corner, (1, SUB, SUB * POLC))
        addend = jnp.where(inside, sub_grids[slot_index], 0.0)[None]
        return lax.dynamic_update_slice(canvas, window + addend, corner)

    return lax.fori_loop(0, sub_grids.shape[0], add_one, canvas)


def rank_within(labels, label_count):
    onehot = (labels[:, None] == jnp.arange(label_count, dtype=jnp.int32)[None, :]).astype(
        jnp.int32
    )
    before = jnp.cumsum(onehot, axis=0) - onehot
    return jnp.sum(before * onehot, axis=1)


def on_device(
    vis_data,
    u_cell,
    v_cell,
    u_frac,
    v_frac,
    w_plane,
    block_route,
    kernel_taps,
    taper_gain,
    sub_tile,
    sub_anchor,
):
    vis_count = lax.axis_size("vis")
    tile_width = lax.axis_size("tile")
    group_size = BLK_DEV * vis_count
    slot_cap = max(2, 2 * ROWS_DEV // group_size)
    row_count = vis_data.shape[0]
    flat_route = block_route[:, 0]
    row_rank = rank_within(flat_route, group_size)
    owner_idx = flat_route // BLK_DEV
    local_idx = flat_route % BLK_DEV
    dest_slot = (local_idx * vis_count + owner_idx) * slot_cap + row_rank
    buffer_rows = BLK_DEV * vis_count * slot_cap
    send_data = jnp.zeros((buffer_rows, CHR * POLC), jnp.bfloat16).at[dest_slot].set(vis_data)
    send_data = send_data.reshape(BLK_DEV, vis_count, slot_cap, CHR * POLC)
    table_u = w_plane * OS + u_frac
    table_v = w_plane * OS + v_frac
    codes_all = jnp.stack([u_cell.T, v_cell.T, table_u.T, table_v.T], axis=1).reshape(
        row_count, 4 * CHR
    )
    code_type = jnp.int32
    send_codes = jnp.zeros((buffer_rows, 4 * CHR), code_type).at[dest_slot].set(codes_all)
    send_codes = send_codes.reshape(BLK_DEV, vis_count, slot_cap, 4 * CHR)

    def grid_one(member):
        samples = member[0].reshape(-1, POLC)
        code_rows = (
            jnp.transpose(member[1].reshape(-1, 4, CHR), (1, 0, 2)).reshape(4, -1).astype(jnp.int32)
        )
        return grid_block(samples, code_rows, kernel_taps, taper_gain)

    subgrids = lax.map(
        grid_one,
        (
            lax.all_to_all(send_data, "vis", split_axis=1, concat_axis=1, tiled=True),
            lax.all_to_all(send_codes, "vis", split_axis=1, concat_axis=1, tiled=True),
        ),
    )
    tile_ids = sub_tile[:, 0]
    per_owner = GT_DEV * SCAP
    tile_rank = rank_within(tile_ids, GT_DEV * tile_width)
    sub_slot = tile_ids // GT_DEV * per_owner + tile_ids % GT_DEV * SCAP + tile_rank
    send_subs = (
        jnp.zeros((tile_width * per_owner, SUB, SUB * POLC), jnp.float32).at[sub_slot].set(subgrids)
    )
    send_anchor = jnp.zeros((tile_width * per_owner, 2), jnp.int32).at[sub_slot].set(sub_anchor)
    moved_subs, moved_anchor = (
        lax.all_to_all(send_subs, "tile", split_axis=0, concat_axis=0, tiled=True),
        lax.all_to_all(send_anchor, "tile", split_axis=0, concat_axis=0, tiled=True),
    )
    local_tiles = jnp.arange(tile_width * per_owner, dtype=jnp.int32) % per_owner // SCAP
    canvas = place_tiles(
        jnp.zeros((GT_DEV, TS, TS * POLC), jnp.float32), moved_subs, local_tiles, moved_anchor, 0
    )
    return lax.psum_scatter(canvas, "vis", scatter_dimension=1, tiled=True)


def solution(mesh):
    placed = (
        P(("vis", "tile"), None),
        P(None, ("vis", "tile")),
        P(None, ("vis", "tile")),
        P(None, ("vis", "tile")),
        P(None, ("vis", "tile")),
        P(None, ("vis", "tile")),
        P(("vis", "tile"), None),
        P(),
        P(),
        P(("vis", "tile"), None),
        P(("vis", "tile"), None),
    )
    return jax.shard_map(
        on_device, mesh=mesh, in_specs=placed, out_specs=P("tile", "vis", None), check_vma=False
    )
```

profile of v0, /device:TPU:0, one launch (start us, length us, event | category | flops | bytes accessed | tf_op | source)
XLA Modules:
  0.0 407.8 jit_solution(5670956929467990750)
XLA Ops:
  9.3 18.0 %reduce-window.6 = s32[64,8,128]{2,1,0:T(8,128)S(1)} reduce-window(s32[64,8,128]{2,1,0:T(8,128)S(1)} %fusion.64, s32[]{:T(128)} %constant.175.clone.1), window={size=1x1x128 pad=0_0x0_0x127_0}, to_apply=%region_3.4 | reduce-window | flops 8323072 | bytes 524292 | tf_op jit(solution)/shard_map/reduce-window
  29.4 3.3 scatter_custom_fusion.1
  34.3 7.3 %all-to-all-start.1 = ((s32[8,1,16384]{2,1,0:T(1,128)}), s32[8,1,16384]{2,1,0:T(1,128)S(1)}, u32[]{:S(2)}, u32[]{:S(2)}) async-start(s32[8,1,16384]{2,1,0:T(1,128)} %reshape.274), calls=%async_computation.1 | async-start | bytes 1048576 | tf_op jit(solution)/shard_map/all_to_all | solution.py:123
  41.5 3.7 scatter_custom_fusion.2
  46.1 10.0 %all-to-all-done.1 = s32[8,1,16384]{2,1,0:T(1,128)S(1)} async-done(((s32[8,1,16384]{2,1,0:T(1,128)}), s32[8,1,16384]{2,1,0:T(1,128)S(1)}, u32[]{:S(2)}, u32[]{:S(2)}) %all-to-all-start.1) | async-done | bytes 524320 | tf_op jit(solution)/shard_map/all_to_all | solution.py:123
  56.0 3.6 all-to-all-start.2
  62.0 1.9 reduce
  64.4 9.9 %all-to-all-done.2 = bf16[8,8,32,128]{3,2,0,1:T(8,128)(2,1)S(1)} async-done(((bf16[8,8,32,128]{3,2,0,1:T(8,128)(2,1)}), bf16[8,8,32,128]{3,2,0,1:T(8,128)(2,1)S(1)}, u32[]{:S(2)}, u32[]{:S(2)}) %all-to-all-start.2) | async-done | bytes 524320 | tf_op jit(solution)/shard_map/all_to_all | solution.py:122
  74.3 3.2 all-to-all-start
  77.6 68.9 %while.23 = (s32[]{:T(128)}, f32[8,32,256]{2,1,0:T(8,128)}, s32[8,8,32,64]{3,2,0,1:T(8,128)S(1)}, f32[128,7]{0,1:T(8,128)S(1)}, bf16[8,8,32,128]{3,2,0,1:T(8,128)(2,1)S(1)}, /*index=5*/f32[32,32]{0,1:T(8,128)S(1)}, s32[]{:T(128)}) while((s32[]{:T(128)}, f32[8,32,256]{2,1,0:T(8,128)}, s32[8,8,32,64]{3,2,0,1:T(8,128)S(1)}, ...), condition=%wide.region_9.10_spmd, body=%wide.region_8.9_spmd.sunk | while | flops 164274176 | bytes 8039577 | solution.py:119
  78.2 1.8 fusion.93
  80.6 1.8 fusion.96
  86.8 1.8 fusion.93
  89.2 1.8 fusion.96
  95.4 1.8 fusion.93
  97.8 1.8 fusion.96
  104.1 1.8 fusion.93
  106.4 1.8 fusion.96
  112.7 1.8 fusion.93
  115.0 1.8 fusion.96
  121.3 1.8 fusion.93
  123.6 1.8 fusion.96
  129.9 1.8 fusion.93
  132.3 1.8 fusion.96
  138.5 1.8 fusion.93
  140.9 1.8 fusion.96
  147.3 2.4 scatter_fusion
  149.8 3.5 all-to-all-start.3
  153.4 8.6 %all-to-all-done.3 = f32[16,32,256]{2,1,0:T(8,128)S(1)} async-done(((f32[16,32,256]{2,1,0:T(8,128)}), f32[16,32,256]{2,1,0:T(8,128)S(1)}, u32[]{:S(2)}, u32[]{:S(2)}) %all-to-all-start.3) | async-done | bytes 524320 | tf_op jit(solution)/shard_map/all_to_all | solution.py:135
  162.0 2.4 broadcast_in_dim.150
  164.5 149.4 %while.24 = (s32[]{:T(128)}, f32[2,256,2048]{2,1,0:T(8,128)}, s32[16]{0:T(128)S(1)}, s32[16,2]{0,1:T(2,128)S(1)}, f32[16,32,256]{2,1,0:T(8,128)S(1)}, /*index=5*...) while((s32[]{:T(128)}, f32[2,256,2048]{2,1,0:T(8,128)}, ...), condition=%wide.region_12.13_spmd, body=%wide.region_11.12_spmd.sunk | while | flops 16398 | bytes 164151 | solution.py:66
  170.9 3.0 dynamic_update_slice.15
  180.4 2.8 dynamic_update_slice.15
  189.6 3.0 dynamic_update_slice.15
  199.1 2.8 dynamic_update_slice.15
  208.4 2.8 dynamic_update_slice.15
  217.6 2.8 dynamic_update_slice.15
  226.9 3.0 dynamic_update_slice.15
  236.4 2.8 dynamic_update_slice.15
  245.6 2.9 dynamic_update_slice.15
  255.1 2.8 dynamic_update_slice.15
  264.3 2.8 dynamic_update_slice.15
  273.6 2.8 dynamic_update_slice.15
  282.9 3.0 dynamic_update_slice.15
  292.3 2.8 dynamic_update_slice.15
  301.6 3.0 dynamic_update_slice.15
  311.0 2.8 dynamic_update_slice.15
  313.9 87.1 %reduce-scatter.2.cloned.1.call-done = f32[2,32,2048]{2,1,0:T(8,128)} async-done(((f32[2,256,2048]{2,1,0:T(8,128)}), f32[2,32,2048]{2,1,0:T(8,128)}) %reduce-scatter.2.cloned.1.call-update) | async-done | bytes 524304 | tf_op jit(solution)/shard_map/reduce_scatter | solution.py:142
  (289 shorter events, 83.5 us)
Async XLA Ops:
  29.3 30.3 %copy-start.4 = (s32[8,2]{0,1:T(2,128)S(1)}, s32[8,2]{0,1:T(2,128)}, u32[]{:S(2)}) copy-start(s32[8,2]{0,1:T(2,128)} %param.25) | copy-start | bytes 196
  29.3 30.4 %copy-start.3 = (s32[8,1]{0,1:T(1,128)S(1)}, s32[8,1]{0,1:T(1,128)}, u32[]{:S(2)}) copy-start(s32[8,1]{0,1:T(1,128)} %param.24) | copy-start | bytes 100
  29.3 32.0 %copy-start.2 = (f32[32,32]{1,0:T(8,128)S(1)}, f32[32,32]{1,0:T(8,128)}, u32[]{:S(2)}) copy-start(f32[32,32]{1,0:T(8,128)} %param.23) | copy-start | bytes 12292
  32.8 44.7 %copy-start.5 = (f32[128,7]{0,1:T(8,128)S(1)}, f32[128,7]{0,1:T(8,128)}, u32[]{:S(2)}) copy-start(f32[128,7]{0,1:T(8,128)} %param.22) | copy-start | bytes 10756
  34.3 21.8 %all-to-all-start.1 = ((s32[8,1,16384]{2,1,0:T(1,128)}), s32[8,1,16384]{2,1,0:T(1,128)S(1)}, u32[]{:S(2)}, u32[]{:S(2)}) async-start(s32[8,1,16384]{2,1,0:T(1,128)} %reshape.274), calls=%async_computation.1 | async-start | bytes 1048576 | tf_op jit(solution)/shard_map/all_to_all | solution.py:123
  56.0 18.3 %all-to-all-start.2 = ((bf16[8,8,32,128]{3,2,0,1:T(8,128)(2,1)}), bf16[8,8,32,128]{3,2,0,1:T(8,128)(2,1)S(1)}, u32[]{:S(2)}, u32[]{:S(2)}) async-start(bf16[8,8,32,128]{3,2,0,1:T(8,128)(2,1)} %copy.58), calls=%async_computation.2 | async-start | bytes 1048576 | tf_op jit(solution)/shard_map/all_to_all | solution.py:122
  74.3 75.4 %all-to-all-start = ((s32[4,4,2]{1,2,0:T(2,128)}), s32[4,4,2]{1,2,0:T(2,128)S(1)}, u32[]{:S(2)}, u32[]{:S(2)}) async-start(s32[4,4,2]{1,2,0:T(2,128)} %copy.52), calls=%async_computation | async-start | bytes 8192 | tf_op jit(solution)/shard_map/all_to_all | solution.py:136
  77.6 5.2 %copy-start = (s32[8,8,32,64]{3,2,0,1:T(8,128)}, s32[8,8,32,64]{3,2,0,1:T(8,128)S(1)}, u32[]{:S(2)}) copy-start(s32[8,8,32,64]{3,2,0,1:T(8,128)S(1)} %get-tuple-element.319) | copy-start | bytes 1572868 | tf_op jit(solution)/shard_map/while
  84.8 1.4 copy-start.1
  86.2 5.2 %copy-start = (s32[8,8,32,64]{3,2,0,1:T(8,128)}, s32[8,8,32,64]{3,2,0,1:T(8,128)S(1)}, u32[]{:S(2)}) copy-start(s32[8,8,32,64]{3,2,0,1:T(8,128)S(1)} %get-tuple-element.319) | copy-start | bytes 1572868 | tf_op jit(solution)/shard_map/while
  93.4 1.4 copy-start.1
  94.8 5.2 %copy-start = (s32[8,8,32,64]{3,2,0,1:T(8,128)}, s32[8,8,32,64]{3,2,0,1:T(8,128)S(1)}, u32[]{:S(2)}) copy-start(s32[8,8,32,64]{3,2,0,1:T(8,128)S(1)} %get-tuple-element.319) | copy-start | bytes 1572868 | tf_op jit(solution)/shard_map/while
  102.0 1.4 copy-start.1
  103.4 5.2 %copy-start = (s32[8,8,32,64]{3,2,0,1:T(8,128)}, s32[8,8,32,64]{3,2,0,1:T(8,128)S(1)}, u32[]{:S(2)}) copy-start(s32[8,8,32,64]{3,2,0,1:T(8,128)S(1)} %get-tuple-element.319) | copy-start | bytes 1572868 | tf_op jit(solution)/shard_map/while
  110.7 1.4 copy-start.1
  112.0 5.2 %copy-start = (s32[8,8,32,64]{3,2,0,1:T(8,128)}, s32[8,8,32,64]{3,2,0,1:T(8,128)S(1)}, u32[]{:S(2)}) copy-start(s32[8,8,32,64]{3,2,0,1:T(8,128)S(1)} %get-tuple-element.319) | copy-start | bytes 1572868 | tf_op jit(solution)/shard_map/while
  119.3 1.4 copy-start.1
  120.6 5.2 %copy-start = (s32[8,8,32,64]{3,2,0,1:T(8,128)}, s32[8,8,32,64]{3,2,0,1:T(8,128)S(1)}, u32[]{:S(2)}) copy-start(s32[8,8,32,64]{3,2,0,1:T(8,128)S(1)} %get-tuple-element.319) | copy-start | bytes 1572868 | tf_op jit(solution)/shard_map/while
  127.9 1.4 copy-start.1
  129.3 5.2 %copy-start = (s32[8,8,32,64]{3,2,0,1:T(8,128)}, s32[8,8,32,64]{3,2,0,1:T(8,128)S(1)}, u32[]{:S(2)}) copy-start(s32[8,8,32,64]{3,2,0,1:T(8,128)S(1)} %get-tuple-element.319) | copy-start | bytes 1572868 | tf_op jit(solution)/shard_map/while
  136.5 1.4 copy-start.1
  137.9 5.2 %copy-start = (s32[8,8,32,64]{3,2,0,1:T(8,128)}, s32[8,8,32,64]{3,2,0,1:T(8,128)S(1)}, u32[]{:S(2)}) copy-start(s32[8,8,32,64]{3,2,0,1:T(8,128)S(1)} %get-tuple-element.319) | copy-start | bytes 1572868 | tf_op jit(solution)/shard_map/while
  145.1 1.4 copy-start.1
  149.8 12.3 %all-to-all-start.3 = ((f32[16,32,256]{2,1,0:T(8,128)}), f32[16,32,256]{2,1,0:T(8,128)S(1)}, u32[]{:S(2)}, u32[]{:S(2)}) async-start(f32[16,32,256]{2,1,0:T(8,128)} %scatter_fusion), calls=%async_computation.3 | async-start | bytes 1048576 | tf_op jit(solution)/shard_map/all_to_all | solution.py:135
  153.2 247.8 %reduce-scatter.2.cloned.1.call-start = ((), (), s32[]{:S(2)}) async-start(), calls=%async_computation.5 | async-start | bytes 4718592 | tf_op jit(solution)/shard_map/reduce_scatter | solution.py:142
Sparse Core Ops, SparseCore 0:
  314.0 86.9 reduce-scatter.1
where the time goes:
time: 414 us; the launch traced here: 408 us
  waiting for transfers between devices  116 us (28%)
  local copies, waits for them, and re-layouts  108 us (26%)
  loops' own time  70.5 us (17%)
  other arithmetic  42.3 us (10%)
  matrix products  40.4 us (10%)
  starting transfers between devices  17.6 us (4%)
  between operations  13.6 us (3%)
    reduce_scatter x1, waiting for transfers between devices, on_device(): return lax.psum_scatter(canvas, 'vis', scatter_dimension=1, tiled=True)  87.1 us
    another operation x1, loops' own time, place_tiles(): return lax.fori_loop(0, sub_grids.shape[0], add_one, canvas)  69.6 us
    dynamic_update_slice x16, local copies, waits for them, and re-layouts, add_one(): return lax.dynamic_update_slice(canvas, window + addend, corner)  45.7 us
    dot_general x16, matrix products, lookup(): return jnp.dot(picker, kernel_taps, precision=lax.Precision.HIGHEST)  29.5 us
    another operation x3, other arithmetic  18.2 us
    add x16, other arithmetic, add_one(): return lax.dynamic_update_slice(canvas, window + addend, corner)  14.8 us
    convert_element_type x16, local copies, waits for them, and re-layouts, grid_block(): samples.astype(jnp.float32)[:, None, :]  13.6 us
    dot_general x8, matrix products, grid_block(): lax.dot_general(weight_v, weighted, (((0,), (0,)), ((), ())), preferred_e...  10.9 us
  transfers between devices with their start and end apart: 5, of which 4 were waited for; matrix products, arithmetic and copies ran while one was open for 20% of the time, Pallas kernels for 0%

commit v1 on v0

v1 whole, which is shorter than its diff:
```python
import functools

import jax
import jax.numpy as jnp
from jax import lax
from jax.experimental import pallas as pl
from jax.experimental.pallas import tpu as pltpu
from jax.sharding import PartitionSpec as P

BLK_DEV = 8
SUB = 32
POLC = 8
TAPS = 7
OS = 16
TS = 256
GT = 8
SCAP = 2
LANES = 128
ROWS = 8
FAR = 1 << 20
NT = (((1,), (1,)), ((), ()))


def dispatch_kernel(
    slot_cap, vis, u_cell, v_cell, u_frac, v_frac, w_plane, route, out, feat, dest
):
    rows = vis.shape[0]
    columns = vis.shape[1]
    channels = u_cell.shape[0]
    owners, _, chunk = out.shape
    groups = owners * BLK_DEV
    feat[pl.ds(0, columns), :] = vis[...].astype(jnp.float32).T.astype(jnp.bfloat16)
    plane = w_plane[...] * OS
    codes = (u_cell[...], v_cell[...], plane + u_frac[...], plane + v_frac[...])
    for place, code in enumerate(codes):
        feat[pl.ds(columns + place * channels, channels), :] = code.astype(jnp.float32).astype(
            jnp.bfloat16
        )
    names = route[...]
    mine = lax.broadcasted_iota(jnp.int32, (groups, rows), 0) == names
    onehot = jnp.where(mine, 1.0, 0.0)
    earlier = lax.broadcasted_iota(jnp.int32, (rows, rows), 0) < lax.broadcasted_iota(
        jnp.int32, (rows, rows), 1
    )
    before = jnp.dot(
        onehot.astype(jnp.bfloat16),
        jnp.where(earlier, 1.0, 0.0).astype(jnp.bfloat16),
        preferred_element_type=jnp.float32,
    )
    rank = jnp.sum(onehot * before, axis=0, keepdims=True).astype(jnp.int32)
    dest[...] = names * slot_cap + rank

    def send(owner, _):
        slots = lax.broadcasted_iota(jnp.int32, (chunk, rows), 0) + owner * chunk
        pick = jnp.where(slots == dest[...], 1.0, 0.0).astype(jnp.bfloat16)
        out[owner] = lax.dot_general(
            feat[...], pick, NT, preferred_element_type=jnp.float32
        ).astype(jnp.bfloat16)
        return 0

    lax.fori_loop(0, owners, send, 0)


def spread(cell, taps, offsets):
    delta = offsets - cell
    weight = jnp.zeros(delta.shape, jnp.float32)
    for tap in range(TAPS):
        weight = jnp.where(delta == tap, taps[tap : tap + 1, :], weight)
    return weight


def grid_kernel(slot_cap, chunk, channels, slot_of, feat, table, taper, out, total, left, right):
    step = pl.program_id(0)
    covered = min(BLK_DEV, LANES // slot_cap)
    first = (step * LANES) % chunk // slot_cap
    columns = channels * POLC

    @pl.when(step == 0)
    def _():
        total[...] = jnp.zeros_like(total)
        out[...] = jnp.zeros_like(out)

    lanes = lax.broadcasted_iota(jnp.int32, (SUB, LANES), 1)
    block = (step * LANES + lanes) % chunk // slot_cap - first
    offsets = lax.broadcasted_iota(jnp.int32, (SUB, LANES), 0)
    samples = feat[0, pl.ds(0, columns), :].astype(jnp.float32)
    codes = feat[0, pl.ds(columns, 4 * channels), :].astype(jnp.float32).astype(jnp.int32)
    lookup = table[...]
    for h in range(channels):
        sample = samples[h * POLC : (h + 1) * POLC, :]
        cell_u = codes[h : h + 1, :]
        cell_v = codes[channels + h : channels + h + 1, :]
        row_u = codes[2 * channels + h : 2 * channels + h + 1, :]
        row_v = codes[3 * channels + h : 3 * channels + h + 1, :]
        taps_u = jnp.take_along_axis(lookup, jnp.broadcast_to(row_u, (8, LANES)), axis=1)
        taps_v = jnp.take_along_axis(lookup, jnp.broadcast_to(row_v, (8, LANES)), axis=1)
        weight_u = spread(cell_u, taps_u, offsets)
        weight_v = spread(cell_v, taps_v, offsets)
        here = pl.ds(h * LANES, LANES)
        weighted = weight_u[:, None, :] * sample[None, :, :]
        right[:, here] = weighted.reshape(SUB * POLC, LANES).astype(jnp.bfloat16)
        for b in range(covered):
            left[pl.ds(b * SUB, SUB), here] = jnp.where(block == b, weight_v, 0.0).astype(
                jnp.bfloat16
            )
    part = lax.dot_general(left[...], right[...], NT, preferred_element_type=jnp.float32)
    place = pl.ds(pl.multiple_of(first * SUB, SUB), covered * SUB)
    total[place, :] = total[place, :] + part

    @pl.when(step == pl.num_programs(0) - 1)
    def _():
        for b in range(BLK_DEV):
            sub = total[pl.ds(b * SUB, SUB), :] * taper[...]
            out[slot_of[b]] = sub.astype(jnp.bfloat16)


def place_kernel(tile_slots, offset_v, offset_u, subs, out, canvas):
    step = pl.program_id(0)
    slots = subs.shape[1]
    height = out.shape[1]
    width = out.shape[2]
    span = SUB * POLC

    @pl.when(step == 0)
    def _():
        canvas[...] = jnp.zeros_like(canvas)

    def add_one(slot, _):
        low = offset_v[step * slots + slot]
        column = offset_u[step * slots + slot]

        @pl.when((low > 0) & (low < height + SUB))
        def _():
            sub = subs[0, slot].astype(jnp.float32)
            sub = jnp.concatenate([sub, jnp.zeros((SUB, LANES), jnp.float32)], axis=1)
            sub = pltpu.roll(sub, column % LANES, 1)
            sub = jnp.concatenate([sub, jnp.zeros((ROWS, span + LANES), jnp.float32)], axis=0)
            sub = pltpu.roll(sub, low % ROWS, 0)
            top = pl.multiple_of(low // ROWS * ROWS, ROWS)
            base = pl.multiple_of(column // LANES * LANES, LANES)
            tile = slot % tile_slots // SCAP
            here = (tile, pl.ds(top, SUB + ROWS), pl.ds(base, span + LANES))
            canvas[here] = canvas[here] + sub

        return 0

    lax.fori_loop(0, slots, add_one, 0)

    @pl.when(step == pl.num_programs(0) - 1)
    def _():
        out[...] = canvas[:, pl.ds(SUB, height), pl.ds(0, width)]


def on_device(
    vis_data,
    u_cell,
    v_cell,
    u_frac,
    v_frac,
    w_plane,
    block_route,
    kernel_taps,
    taper_gain,
    sub_tile,
    sub_anchor,
):
    vis_count = lax.axis_size("vis")
    tile_width = lax.axis_size("tile")
    gt_dev = GT // tile_width
    rows, columns = vis_data.shape
    channels = u_cell.shape[0]
    slot_cap = max(2, 2 * rows // (BLK_DEV * vis_count))
    chunk = BLK_DEV * slot_cap
    features = columns + 4 * channels
    per_owner = gt_dev * SCAP
    slots = tile_width * per_owner
    height = TS // vis_count
    width = TS * POLC

    meta = jnp.concatenate([sub_tile, sub_anchor], axis=1)
    meta = lax.all_gather(meta, ("vis", "tile"), axis=0, tiled=True)
    meta = meta.reshape(vis_count * tile_width, BLK_DEV, 3)
    order = jnp.arange(BLK_DEV, dtype=jnp.int32)

    def ranks(tiles):
        same = tiles[..., :, None] == tiles[..., None, :]
        return jnp.sum((same & (order[None, :] < order[:, None])).astype(jnp.int32), axis=-1)

    wanted = jnp.arange(per_owner, dtype=jnp.int32)
    tiles_all = meta[:, :, 0]
    slot_all = (tiles_all - lax.axis_index("tile") * gt_dev) * SCAP + ranks(tiles_all)
    hit = slot_all[:, None, :] == wanted[None, :, None]
    low = jnp.sum(jnp.where(hit, meta[:, None, :, 1] + FAR, 0), axis=-1) - FAR
    offset_v = (low - lax.axis_index("vis") * height + SUB).reshape(-1)
    offset_u = jnp.sum(jnp.where(hit, meta[:, None, :, 2], 0), axis=-1).reshape(-1) * POLC

    send = pl.pallas_call(
        functools.partial(dispatch_kernel, slot_cap),
        out_shape=jax.ShapeDtypeStruct((vis_count, features, chunk), jnp.bfloat16),
        scratch_shapes=[
            pltpu.VMEM((features, rows), jnp.bfloat16),
            pltpu.VMEM((1, rows), jnp.int32),
        ],
        name="dispatch",
    )(vis_data, u_cell, v_cell, u_frac, v_frac, w_plane, block_route.reshape(1, rows))
    moved = lax.all_to_all(send, "vis", split_axis=0, concat_axis=0, tiled=True)
    if chunk % LANES:
        moved = jnp.transpose(moved, (1, 0, 2)).reshape(1, features, vis_count * chunk)
    per_source = moved.shape[2] // LANES
    steps = moved.shape[0] * per_source
    covered = min(BLK_DEV, LANES // slot_cap)

    table = jnp.pad(kernel_taps.astype(jnp.bfloat16).astype(jnp.float32).T, ((0, 8 - TAPS), (0, 0)))
    taper = jnp.repeat(taper_gain, POLC, axis=1)
    tile_ids = sub_tile[:, 0]
    slot_of = tile_ids * SCAP + ranks(tile_ids)
    subs = pl.pallas_call(
        functools.partial(grid_kernel, slot_cap, chunk, channels),
        grid_spec=pltpu.PrefetchScalarGridSpec(
            num_scalar_prefetch=1,
            grid=(steps,),
            in_specs=[
                pl.BlockSpec(
                    (1, features, LANES), lambda s, *_: (s // per_source, 0, s % per_source)
                ),
                pl.BlockSpec(table.shape, lambda s, *_: (0, 0)),
                pl.BlockSpec(taper.shape, lambda s, *_: (0, 0)),
            ],
            out_specs=pl.BlockSpec((slots, SUB, SUB * POLC), lambda s, *_: (0, 0, 0)),
            scratch_shapes=[
                pltpu.VMEM((BLK_DEV * SUB, SUB * POLC), jnp.float32),
                pltpu.VMEM((covered * SUB, channels * LANES), jnp.bfloat16),
                pltpu.VMEM((SUB * POLC, channels * LANES), jnp.bfloat16),
            ],
        ),
        out_shape=jax.ShapeDtypeStruct((slots, SUB, SUB * POLC), jnp.bfloat16),
        name="grid",
    )(slot_of, moved, table, taper)
    subs = lax.all_to_all(subs, "tile", split_axis=0, concat_axis=0, tiled=True)
    subs = lax.all_gather(subs, "vis", axis=0)
    return pl.pallas_call(
        functools.partial(place_kernel, per_owner),
        grid_spec=pltpu.PrefetchScalarGridSpec(
            num_scalar_prefetch=2,
            grid=(vis_count,),
            in_specs=[pl.BlockSpec((1, slots, SUB, SUB * POLC), lambda s, *_: (s, 0, 0, 0))],
            out_specs=pl.BlockSpec((gt_dev, height, width), lambda s, *_: (0, 0, 0)),
            scratch_shapes=[
                pltpu.VMEM((gt_dev, -(-height // ROWS) * ROWS + 2 * SUB + ROWS, width + LANES), jnp.float32),
            ],
        ),
        out_shape=jax.ShapeDtypeStruct((gt_dev, height, width), jnp.float32),
        name="place",
    )(offset_v, offset_u, subs)


def solution(mesh):
    placed = (
        P(("vis", "tile"), None),
        P(None, ("vis", "tile")),
        P(None, ("vis", "tile")),
        P(None, ("vis", "tile")),
        P(None, ("vis", "tile")),
        P(None, ("vis", "tile")),
        P(("vis", "tile"), None),
        P(),
        P(),
        P(("vis", "tile"), None),
        P(("vis", "tile"), None),
    )
    return jax.shard_map(
        on_device, mesh=mesh, in_specs=placed, out_specs=P("tile", "vis", None), check_vma=False
    )
```

time: 414 us -> 135 us (0.33); the launches traced: 408 us -> 134 us
  local copies, waits for them, and re-layouts: 108 us -> 3.33 us
  waiting for transfers between devices: 116 us -> 24.3 us
  loops' own time: 70.5 us -> 0 us
  blocking collectives: 0 us -> 49.2 us
  other arithmetic: 42.3 us -> 1.54 us
  matrix products: 40.4 us -> 0 us
  Pallas kernels: 0 us -> 34.7 us
  starting transfers between devices: 17.6 us -> 7.46 us
    reduce_scatter x1 -> x0, waiting for transfers between devices: 87.1 us -> none  [on_device(): return lax.psum_scatter(canvas, 'vis', scatter_dimension=1, tiled=True)]
    another operation x2 -> x0, loops' own time: 70.5 us -> none  [the longest x1 69.6 us: place_tiles(): return lax.fori_loop(0, sub_grids.shape[0], add_one, canvas)]
    dynamic_update_slice x16 -> x0, local copies, waits for them, and re-layouts: 45.7 us -> none  [add_one(): return lax.dynamic_update_slice(canvas, window + addend, corner)]
    dot_general x24 -> x0, matrix products: 40.4 us -> none  [the longest x16 29.5 us: lookup(): return jnp.dot(picker, kernel_taps, precision=lax.Precision.HIGHEST)]
    all_gather x0 -> x1, blocking collectives: none -> 39.1 us  [on_device(): meta = lax.all_gather(meta, ('vis', 'tile'), axis=0, tiled=True)]
    pallas_call x0 -> x3, Pallas kernels: none -> 34.7 us  [the longest x1 22.5 us: on_device(): pl.pallas_call(functools.partial(grid_kernel, slot_cap, chunk, channels),...]
    dynamic_slice x48 -> x0, local copies, waits for them, and re-layouts: 20.6 us -> none  [the longest x16 9.96 us: add_one(): anchors[slot_index, 1] * POLC]
    another operation x6 -> x0, other arithmetic: 20 us -> none
  transfers between devices with their start and end apart: 5 -> 2, of which waited for: 4 -> 2; matrix products, arithmetic and copies ran while one was open for 20% -> 3% of each run, Pallas kernels for 0% -> 0%
where the time goes in v1:
time: 135 us; the launch traced here: 134 us
  blocking collectives  49.2 us (36%)
  Pallas kernels  34.7 us (26%)
  waiting for transfers between devices  24.3 us (18%)
  between operations  13.5 us (10%)
  starting transfers between devices  7.46 us (6%)
  local copies, waits for them, and re-layouts  3.33 us (2%)
  other arithmetic  1.54 us (1%)
    all_gather x1, blocking collectives, on_device(): meta = lax.all_gather(meta, ('vis', 'tile'), axis=0, tiled=True)  39.1 us
    pallas_call x1, Pallas kernels, on_device(): pl.pallas_call(functools.partial(grid_kernel, slot_cap, chunk, channels),...  22.5 us
    all_to_all x1, waiting for transfers between devices, on_device(): moved = lax.all_to_all(send, 'vis', split_axis=0, concat_axis=0, tiled=True)  18 us
    all_to_all x1, blocking collectives, on_device(): subs = lax.all_to_all(subs, 'tile', split_axis=0, concat_axis=0, tiled=True)  10.1 us
    all_to_all x1, starting transfers between devices, on_device(): moved = lax.all_to_all(send, 'vis', split_axis=0, concat_axis=0, tiled=True)  7.42 us
    pallas_call x1, Pallas kernels, on_device(): pl.pallas_call(functools.partial(place_kernel, per_owner), grid_spec=pltp...  6.84 us
    all_gather x1, waiting for transfers between devices, on_device(): subs = lax.all_gather(subs, 'vis', axis=0)  6.32 us
    pallas_call x1, Pallas kernels, on_device(): pl.pallas_call(functools.partial(dispatch_kernel, slot_cap), out_shape=ja...  5.32 us
  transfers between devices with their start and end apart: 2, of which 2 were waited for; matrix products, arithmetic and copies ran while one was open for 3% of the time, Pallas kernels for 0%

profile of v1, /device:TPU:0, one launch (start us, length us, event | category | flops | bytes accessed | tf_op | source)
XLA Modules:
  0.0 134.0 jit_solution(11390067716266909420)
XLA Ops:
  6.5 0.0 copy-start.1
  6.5 0.0 copy-start.2
  6.5 0.0 copy-start.4
  6.5 5.3 %dispatch.1 = bf16[8,192,256]{2,1,0:T(8,128)(2,1)} custom-call(bf16[1024,128]{1,0:T(8,128)(2,1)} %vis.1, s32[16,1024]{1,0:T(8,128)} %u_cell.1, s32[16,1024]{1,0:T(8,128)} %v_cell.1, s32[16,1024]{1,0:T(8,128)} %u_frac.1, s32[16,1024]{1,0:T(8,128)} %v_frac.1, s32[16,1024]{1,0:T(8,128)} %w_plane.1, s32[1,1024]{1,0:T(1,128)} %bitcast.18), custom_call_target="tpu_custom_call" | custom-call | tf_op jit(solution)/shard_map/dispatch/pallas_call | solution.py:197
  11.9 0.0 copy-start.3
  11.9 7.4 %all-to-all-start = ((bf16[8,192,256]{2,1,0:T(8,128)(2,1)}), bf16[8,192,256]{2,1,0:T(8,128)(2,1)S(1)}, u32[]{:S(2)}, u32[]{:S(2)}) async-start(bf16[8,192,256]{2,1,0:T(8,128)(2,1)} %dispatch.1), calls=%async_computation | async-start | bytes 1572864 | tf_op jit(solution)/shard_map/all_to_all | solution.py:206
  19.3 0.0 all-gather.4.cloned.1.call-start
  19.3 0.0 copy-done.1
  19.3 0.1 copy.21
  19.4 0.7 copy.22.taper
  20.1 0.0 copy-done.2
  20.1 0.6 pad_convert_fusion.table
  20.7 0.0 copy-done.4
  20.7 0.2 convert_reduce_fusion.1
  20.9 0.6 multiply_add_fusion.1.slot_of
  21.5 18.0 %all-to-all-done.feat = bf16[8,192,256]{2,1,0:T(8,128)(2,1)S(1)} async-done(((bf16[8,192,256]{2,1,0:T(8,128)(2,1)}), bf16[8,192,256]{2,1,0:T(8,128)(2,1)S(1)}, u32[]{:S(2)}, u32[]{:S(2)}) %all-to-all-start) | async-done | bytes 786464 | tf_op jit(solution)/shard_map/all_to_all | solution.py:206
  39.5 0.0 copy-start
  39.5 0.9 copy-done
  40.3 22.5 %grid.1 = bf16[16,32,256]{2,1,0:T(8,128)(2,1)} custom-call(s32[8]{0:T(128)} %multiply_add_fusion.1.slot_of, bf16[8,192,256]{2,1,0:T(8,128)(2,1)} %copy-done, f32[8,128]{1,0:T(8,128)} %pad_convert_fusion.table, f32[32,256]{1,0:T(8,128)} %copy.22.taper), custom_call_target="tpu_custom_call" | custom-call | tf_op jit(solution)/shard_map/grid/pallas_call | solution.py:217
  62.8 10.1 %all_to_all.10 = bf16[16,32,256]{2,1,0:T(8,128)(2,1)} all-to-all(bf16[16,32,256]{2,1,0:T(8,128)(2,1)} %grid.1), channel_id=1, replica_groups=mesh['vis'=8,'tile'=4] {'tile'}, dimensions={0} | all-to-all | bytes 524288 | tf_op jit(solution)/shard_map/all_to_all | solution.py:239
  72.9 0.0 all-gather.4.cloned.1.call-update
  73.0 0.0 copy-done.3
  73.0 39.1 %all-gather.1 = s32[32,8,3]{1,2,0:T(4,128)S(1)} all-gather(s32[1,8,3]{1,2,0:T(4,128)S(1)} %add_bitcast_fusion), channel_id=1, replica_groups=mesh['vis'=8,'tile'=4] {'vis','tile'}, dimensions={0}, use_global_device_ids=true | all-gather | bytes 3168 | tf_op jit(solution)/shard_map/all_gather | solution.py:181
  112.2 0.1 copy.17
  112.2 0.1 copy.23
  112.3 0.1 copy.19
  112.4 0.1 convert_reduce_fusion
  112.5 0.1 copy.18
  112.6 0.7 add.45.offset_v
  113.3 0.1 copy.20
  113.4 0.6 mul.33.offset_u
  114.0 6.3 %all-gather.4.cloned.1.call-done = bf16[128,32,256]{2,1,0:T(8,128)(2,1)} async-done(((bf16[16,32,256]{2,1,0:T(8,128)(2,1)}), bf16[128,32,256]{2,1,0:T(8,128)(2,1)}) %all-gather.4.cloned.1.call-update) | async-done | bytes 2097168 | tf_op jit(solution)/shard_map/all_gather | solution.py:240
  120.4 6.8 %place.1 = f32[2,32,2048]{2,1,0:T(8,128)} custom-call(s32[128]{0:T(128)} %add.45.offset_v, s32[128]{0:T(128)} %mul.33.offset_u, bf16[8,16,32,256]{3,2,1,0:T(8,128)(2,1)} %bitcast.14), custom_call_target="tpu_custom_call" | custom-call | tf_op jit(solution)/shard_map/place/pallas_call | solution.py:241
  (8 shorter events, 0.1 us)
Async XLA Ops:
  6.5 12.8 %copy-start.1 = (f32[32,32]{1,0:T(8,128)S(1)}, f32[32,32]{1,0:T(8,128)}, u32[]{:S(2)}) copy-start(f32[32,32]{1,0:T(8,128)} %param.19) | copy-start | bytes 12292
  6.5 13.6 %copy-start.2 = (f32[128,7]{0,1:T(8,128)S(1)}, f32[128,7]{0,1:T(8,128)}, u32[]{:S(2)}) copy-start(f32[128,7]{0,1:T(8,128)} %param.18) | copy-start | bytes 10756
  6.5 14.2 %copy-start.4 = (s32[8,1]{0,1:T(1,128)S(1)}, s32[8,1]{0,1:T(1,128)}, u32[]{:S(2)}) copy-start(s32[8,1]{0,1:T(1,128)} %param.20) | copy-start | bytes 100
  11.9 61.1 %copy-start.3 = (s32[8,2]{0,1:T(2,128)S(1)}, s32[8,2]{0,1:T(2,128)}, u32[]{:S(2)}) copy-start(s32[8,2]{0,1:T(2,128)} %param.21) | copy-start | bytes 196
  11.9 27.6 %all-to-all-start = ((bf16[8,192,256]{2,1,0:T(8,128)(2,1)}), bf16[8,192,256]{2,1,0:T(8,128)(2,1)S(1)}, u32[]{:S(2)}, u32[]{:S(2)}) async-start(bf16[8,192,256]{2,1,0:T(8,128)(2,1)} %dispatch.1), calls=%async_computation | async-start | bytes 1572864 | tf_op jit(solution)/shard_map/all_to_all | solution.py:206
  19.3 101.1 %all-gather.4.cloned.1.call-start = ((), (), s32[]{:S(2)}) async-start(), calls=%async_computation.2 | async-start | bytes 2359296 | tf_op jit(solution)/shard_map/all_gather | solution.py:240
  39.5 0.9 copy-start
Sparse Core Ops, SparseCore 0:
  73.1 47.2 all-gather.3

commit v2 on v1

--- a/solution.py
+++ b/solution.py
@@ -18,6 +18,7 @@
 LANES = 128
 ROWS = 8
 FAR = 1 << 20
+MESH = pl.DeviceIdType.MESH
 NT = (((1,), (1,)), ((), ()))
 
 
@@ -114,6 +115,104 @@
             out[slot_of[b]] = sub.astype(jnp.bfloat16)
 
 
+def gather_kernel(subs, meta, out, meta_out, own_sem, near_send, near_recv, far_send, far_recv):
+    count = out.shape[0]
+    width = out.shape[1]
+    v, t = lax.axis_index("vis"), lax.axis_index("tile")
+    half = count // 2
+    spot = v // 2 * (1 - v % 2) + (count - 1 - v // 2) * (v % 2)
+
+    def member(position):
+        position = (position + 2 * count) % count
+        back = position // half
+        return (1 - back) * 2 * position + back * (2 * (count - 1 - position) + 1)
+
+    barrier = pltpu.get_barrier_semaphore()
+    for side in (1, -1):
+        pl.semaphore_signal(
+            barrier, inc=1, device_id=(member(spot + side), t), device_id_type=MESH
+        )
+    for k in range(1, width):
+        pl.semaphore_signal(barrier, inc=1, device_id=(v, (t + k) % width), device_id_type=MESH)
+    pl.semaphore_wait(barrier, 1 + width)
+
+    def near(k):
+        chunk = pl.ds((t + k) % width, 1)
+        pairs = ((subs.at[chunk], out.at[v, pl.ds(t, 1)]), (meta, meta_out.at[v, t]))
+        return [
+            pltpu.make_async_remote_copy(
+                src_ref=src,
+                dst_ref=dst,
+                send_sem=near_send.at[2 * k + i],
+                recv_sem=near_recv.at[2 * k + i],
+                device_id=(v, (t + k) % width),
+                device_id_type=MESH,
+            )
+            for i, (src, dst) in enumerate(pairs)
+        ]
+
+    def own():
+        pairs = ((subs.at[pl.ds(t, 1)], out.at[v, pl.ds(t, 1)]), (meta, meta_out.at[v, t]))
+        return [
+            pltpu.make_async_copy(src, dst, own_sem.at[i]) for i, (src, dst) in enumerate(pairs)
+        ]
+
+    def far(k, step):
+        side = 1 - 2 * (k % 2)
+        origin = member(spot - side * step)
+        source = (t + width - k) % width
+        refs = (out.at[origin, pl.ds(source, 1)], meta_out.at[origin, source])
+        return [
+            pltpu.make_async_remote_copy(
+                src_ref=ref,
+                dst_ref=ref,
+                send_sem=far_send.at[(step * width + k) * 2 + i],
+                recv_sem=far_recv.at[(step * width + k) * 2 + i],
+                device_id=(member(spot + side), t),
+                device_id_type=MESH,
+            )
+            for i, ref in enumerate(refs)
+        ]
+
+    for copy in own():
+        copy.start()
+    for k in range(1, width):
+        for copy in near(k):
+            copy.start()
+    for copy in own():
+        copy.wait()
+    for k in range(width):
+        if k:
+            for copy in near(k):
+                copy.wait_recv()
+        for copy in far(k, 0):
+            copy.start()
+
+    def forward(step, _):
+        for k in range(width):
+            for copy in far(k, step - 1):
+                copy.wait_recv()
+            for copy in far(k, step):
+                copy.start()
+        return 0
+
+    lax.fori_loop(1, count - 1, forward, 0)
+    for k in range(width):
+        for copy in far(k, count - 2):
+            copy.wait_recv()
+    for k in range(1, width):
+        for copy in near(k):
+            copy.wait_send()
+
+    def sent(step, _):
+        for k in range(width):
+            for copy in far(k, step):
+                copy.wait_send()
+        return 0
+
+    lax.fori_loop(0, count - 1, sent, 0)
+
+
 def place_kernel(tile_slots, offset_v, offset_u, subs, out, canvas):
     step = pl.program_id(0)
     slots = subs.shape[1]
@@ -177,22 +276,11 @@
     height = TS // vis_count
     width = TS * POLC
 
-    meta = jnp.concatenate([sub_tile, sub_anchor], axis=1)
-    meta = lax.all_gather(meta, ("vis", "tile"), axis=0, tiled=True)
-    meta = meta.reshape(vis_count * tile_width, BLK_DEV, 3)
     order = jnp.arange(BLK_DEV, dtype=jnp.int32)
 
     def ranks(tiles):
         same = tiles[..., :, None] == tiles[..., None, :]
         return jnp.sum((same & (order[None, :] < order[:, None])).astype(jnp.int32), axis=-1)
-
-    wanted = jnp.arange(per_owner, dtype=jnp.int32)
-    tiles_all = meta[:, :, 0]
-    slot_all = (tiles_all - lax.axis_index("tile") * gt_dev) * SCAP + ranks(tiles_all)
-    hit = slot_all[:, None, :] == wanted[None, :, None]
-    low = jnp.sum(jnp.where(hit, meta[:, None, :, 1] + FAR, 0), axis=-1) - FAR
-    offset_v = (low - lax.axis_index("vis") * height + SUB).reshape(-1)
-    offset_u = jnp.sum(jnp.where(hit, meta[:, None, :, 2], 0), axis=-1).reshape(-1) * POLC
 
     send = pl.pallas_call(
         functools.partial(dispatch_kernel, slot_cap),
@@ -236,8 +324,41 @@
         out_shape=jax.ShapeDtypeStruct((slots, SUB, SUB * POLC), jnp.bfloat16),
         name="grid",
     )(slot_of, moved, table, taper)
-    subs = lax.all_to_all(subs, "tile", split_axis=0, concat_axis=0, tiled=True)
-    subs = lax.all_gather(subs, "vis", axis=0)
+    meta = jnp.concatenate([tile_ids, sub_anchor[:, 0], sub_anchor[:, 1]])
+    meta = jnp.pad(meta, (0, LANES - meta.shape[0])).reshape(1, LANES)
+    hops = (vis_count - 1) * tile_width * 2
+    vmem = pl.BlockSpec(memory_space=pltpu.VMEM)
+    subs, meta = pl.pallas_call(
+        gather_kernel,
+        in_specs=[vmem, vmem],
+        out_specs=[vmem, vmem],
+        out_shape=[
+            jax.ShapeDtypeStruct(
+                (vis_count, tile_width, per_owner, SUB, SUB * POLC), jnp.bfloat16
+            ),
+            jax.ShapeDtypeStruct((vis_count, tile_width, 1, LANES), jnp.int32),
+        ],
+        scratch_shapes=[
+            pltpu.SemaphoreType.DMA((2,)),
+            pltpu.SemaphoreType.DMA((2 * tile_width,)),
+            pltpu.SemaphoreType.DMA((2 * tile_width,)),
+            pltpu.SemaphoreType.DMA((hops,)),
+            pltpu.SemaphoreType.DMA((hops,)),
+        ],
+        compiler_params=pltpu.CompilerParams(collective_id=0, has_side_effects=True),
+        name="gather",
+    )(subs.reshape(tile_width, per_owner, SUB, SUB * POLC), meta)
+    subs = subs.reshape(vis_count, slots, SUB, SUB * POLC)
+    meta = meta.reshape(vis_count * tile_width, LANES)[:, : 3 * BLK_DEV]
+    meta = meta.reshape(vis_count * tile_width, 3, BLK_DEV)
+
+    wanted = jnp.arange(per_owner, dtype=jnp.int32)
+    tiles_all = meta[:, 0]
+    slot_all = (tiles_all - lax.axis_index("tile") * gt_dev) * SCAP + ranks(tiles_all)
+    hit = slot_all[:, None, :] == wanted[None, :, None]
+    low = jnp.sum(jnp.where(hit, meta[:, 1][:, None] + FAR, 0), axis=-1) - FAR
+    offset_v = (low - lax.axis_index("vis") * height + SUB).reshape(-1)
+    offset_u = jnp.sum(jnp.where(hit, meta[:, 2][:, None], 0), axis=-1).reshape(-1) * POLC
     return pl.pallas_call(
         functools.partial(place_kernel, per_owner),
         grid_spec=pltpu.PrefetchScalarGridSpec(

time: 135 us -> 102 us (0.76)
  blocking collectives: 49.2 us -> 0 us
  Pallas kernels: 34.7 us -> 70.3 us
  between operations: 13.5 us -> 0.06 us
  waiting for transfers between devices: 24.3 us -> 17.4 us
    all_gather x1 -> x0, blocking collectives: 39.1 us -> none  [on_device(): meta = lax.all_gather(meta, ('vis', 'tile'), axis=0, tiled=True)]
    pallas_call x0 -> x1, Pallas kernels: none -> 35.3 us  [on_device(): pl.pallas_call(gather_kernel, in_specs=[vmem, vmem], out_specs=[vmem, vme...]
    all_to_all x1 -> x0, blocking collectives: 10.1 us -> none  [on_device(): subs = lax.all_to_all(subs, 'tile', split_axis=0, concat_axis=0, tiled=True)]
    all_gather x1 -> x0, waiting for transfers between devices: 6.32 us -> none  [on_device(): subs = lax.all_gather(subs, 'vis', axis=0)]
  transfers between devices with their start and end apart: 2 -> 1, of which waited for: 2 -> 1; matrix products, arithmetic and copies ran while one was open for 3% -> 3% of each run, Pallas kernels for 0% -> 0%
where the time goes in v2:
time: 102 us; the launch traced here: 101 us
  Pallas kernels  70.3 us (69%)
  waiting for transfers between devices  17.4 us (17%)
  starting transfers between devices  7.3 us (7%)
  local copies, waits for them, and re-layouts  4.43 us (4%)
  other arithmetic  1.53 us (2%)
    pallas_call x1, Pallas kernels, on_device(): pl.pallas_call(gather_kernel, in_specs=[vmem, vmem], out_specs=[vmem, vme...  35.3 us
    pallas_call x1, Pallas kernels, on_device(): pl.pallas_call(functools.partial(grid_kernel, slot_cap, chunk, channels),...  22.5 us
    all_to_all x1, waiting for transfers between devices, on_device(): moved = lax.all_to_all(send, 'vis', split_axis=0, concat_axis=0, tiled=True)  17.4 us
    all_to_all x1, starting transfers between devices, on_device(): moved = lax.all_to_all(send, 'vis', split_axis=0, concat_axis=0, tiled=True)  7.3 us
    pallas_call x1, Pallas kernels, on_device(): pl.pallas_call(functools.partial(place_kernel, per_owner), grid_spec=pltp...  7.18 us
    pallas_call x1, Pallas kernels, on_device(): pl.pallas_call(functools.partial(dispatch_kernel, slot_cap), out_shape=ja...  5.33 us
  transfers between devices with their start and end apart: 1, of which 1 were waited for; matrix products, arithmetic and copies ran while one was open for 3% of the time, Pallas kernels for 0%

profile of v2, /device:TPU:0, one launch (start us, length us, event | category | flops | bytes accessed | tf_op | source)
XLA Modules:
  0.0 101.1 jit_solution(9041674480156089507)
XLA Ops:
  0.0 0.0 copy-start.1
  0.0 0.0 copy-start.3
  0.0 0.0 copy-start.4
  0.0 0.0 copy-start.2
  0.0 5.3 %dispatch.1 = bf16[8,192,256]{2,1,0:T(8,128)(2,1)} custom-call(bf16[1024,128]{1,0:T(8,128)(2,1)} %vis.1, s32[16,1024]{1,0:T(8,128)} %u_cell.1, s32[16,1024]{1,0:T(8,128)} %v_cell.1, s32[16,1024]{1,0:T(8,128)} %u_frac.1, s32[16,1024]{1,0:T(8,128)} %v_frac.1, s32[16,1024]{1,0:T(8,128)} %w_plane.1, s32[1,1024]{1,0:T(1,128)} %bitcast.35), custom_call_target="tpu_custom_call" | custom-call | tf_op jit(solution)/shard_map/dispatch/pallas_call | solution.py:285
  5.3 7.3 %all-to-all-start = ((bf16[8,192,256]{2,1,0:T(8,128)(2,1)}), bf16[8,192,256]{2,1,0:T(8,128)(2,1)S(1)}, u32[]{:S(2)}, u32[]{:S(2)}) async-start(bf16[8,192,256]{2,1,0:T(8,128)(2,1)} %dispatch.1), calls=%async_computation | async-start | bytes 1572864 | tf_op jit(solution)/shard_map/all_to_all | solution.py:294
  12.6 0.0 copy-done.1
  12.6 0.1 copy.20
  12.7 0.7 copy.21.taper
  13.4 0.0 copy-done.3
  13.4 0.0 copy-done.4
  13.4 0.1 pad_add_fusion
  13.5 0.5 pad_bitcast_fusion.meta
  14.0 0.0 copy-done.2
  14.1 0.6 pad_convert_fusion.table
  14.6 0.2 convert_reduce_fusion.1
  14.8 0.5 multiply_add_fusion.slot_of
  15.4 17.4 %all-to-all-done.feat = bf16[8,192,256]{2,1,0:T(8,128)(2,1)S(1)} async-done(((bf16[8,192,256]{2,1,0:T(8,128)(2,1)}), bf16[8,192,256]{2,1,0:T(8,128)(2,1)S(1)}, u32[]{:S(2)}, u32[]{:S(2)}) %all-to-all-start) | async-done | bytes 786464 | tf_op jit(solution)/shard_map/all_to_all | solution.py:294
  32.8 0.0 copy-start
  32.8 0.9 copy-done
  33.7 22.5 %grid.1 = bf16[16,32,256]{2,1,0:T(8,128)(2,1)} custom-call(s32[8]{0:T(128)} %multiply_add_fusion.slot_of, bf16[8,192,256]{2,1,0:T(8,128)(2,1)} %copy-done, f32[8,128]{1,0:T(8,128)} %pad_convert_fusion.table, f32[32,256]{1,0:T(8,128)} %copy.21.taper), custom_call_target="tpu_custom_call" | custom-call | tf_op jit(solution)/shard_map/grid/pallas_call | solution.py:305
  56.2 35.3 %gather.1 = (bf16[8,4,4,32,256]{4,3,2,1,0:T(8,128)(2,1)}, s32[8,4,1,128]{3,2,1,0:T(1,128)}) custom-call(bf16[4,4,32,256]{3,2,1,0:T(8,128)(2,1)} %bitcast.31, s32[1,128]{1,0:T(1,128)} %pad_bitcast_fusion.meta), custom_call_target="tpu_custom_call" | custom-call | tf_op jit(solution)/shard_map/gather/pallas_call | solution.py:331
  91.5 0.8 copy.25
  92.3 0.1 convert_reduce_fusion
  92.5 0.1 copy.23
  92.6 0.7 add.36.offset_v
  93.2 0.1 copy.24
  93.3 0.6 mul.31.offset_u
  93.9 7.2 %place.1 = f32[2,32,2048]{2,1,0:T(8,128)} custom-call(s32[128]{0:T(128)} %add.36.offset_v, s32[128]{0:T(128)} %mul.31.offset_u, bf16[8,16,32,256]{3,2,1,0:T(8,128)(2,1)} %bitcast.30), custom_call_target="tpu_custom_call" | custom-call | tf_op jit(solution)/shard_map/place/pallas_call | solution.py:362
  (8 shorter events, 0.1 us)
Async XLA Ops:
  0.0 12.6 %copy-start.1 = (f32[32,32]{1,0:T(8,128)S(1)}, f32[32,32]{1,0:T(8,128)}, u32[]{:S(2)}) copy-start(f32[32,32]{1,0:T(8,128)} %param.19) | copy-start | bytes 12292
  0.0 13.4 %copy-start.3 = (s32[8,2]{0,1:T(2,128)S(1)}, s32[8,2]{0,1:T(2,128)}, u32[]{:S(2)}) copy-start(s32[8,2]{0,1:T(2,128)} %param.21) | copy-start | bytes 196
  0.0 13.4 %copy-start.4 = (s32[8,1]{0,1:T(1,128)S(1)}, s32[8,1]{0,1:T(1,128)}, u32[]{:S(2)}) copy-start(s32[8,1]{0,1:T(1,128)} %param.20) | copy-start | bytes 100
  0.0 14.0 %copy-start.2 = (f32[128,7]{0,1:T(8,128)S(1)}, f32[128,7]{0,1:T(8,128)}, u32[]{:S(2)}) copy-start(f32[128,7]{0,1:T(8,128)} %param.18) | copy-start | bytes 10756
  5.3 27.5 %all-to-all-start = ((bf16[8,192,256]{2,1,0:T(8,128)(2,1)}), bf16[8,192,256]{2,1,0:T(8,128)(2,1)S(1)}, u32[]{:S(2)}, u32[]{:S(2)}) async-start(bf16[8,192,256]{2,1,0:T(8,128)(2,1)} %dispatch.1), calls=%async_computation | async-start | bytes 1572864 | tf_op jit(solution)/shard_map/all_to_all | solution.py:294
  32.8 0.9 copy-start

commit v3 on v2

--- a/solution.py
+++ b/solution.py
@@ -70,22 +70,15 @@
     return weight
 
 
-def grid_kernel(slot_cap, chunk, channels, slot_of, feat, table, taper, out, total, left, right):
-    step = pl.program_id(0)
+def grid_chunk(slot_cap, chunk, channels, lane, feat, table, total, left, right):
     covered = min(BLK_DEV, LANES // slot_cap)
-    first = (step * LANES) % chunk // slot_cap
+    first = lane % chunk // slot_cap
     columns = channels * POLC
-
-    @pl.when(step == 0)
-    def _():
-        total[...] = jnp.zeros_like(total)
-        out[...] = jnp.zeros_like(out)
-
     lanes = lax.broadcasted_iota(jnp.int32, (SUB, LANES), 1)
-    block = (step * LANES + lanes) % chunk // slot_cap - first
+    block = (lane + lanes) % chunk // slot_cap - first
     offsets = lax.broadcasted_iota(jnp.int32, (SUB, LANES), 0)
-    samples = feat[0, pl.ds(0, columns), :].astype(jnp.float32)
-    codes = feat[0, pl.ds(columns, 4 * channels), :].astype(jnp.float32).astype(jnp.int32)
+    samples = feat[:columns, :].astype(jnp.float32)
+    codes = feat[columns:, :].astype(jnp.float32).astype(jnp.int32)
     lookup = table[...]
     for h in range(channels):
         sample = samples[h * POLC : (h + 1) * POLC, :]
@@ -108,11 +101,87 @@
     place = pl.ds(pl.multiple_of(first * SUB, SUB), covered * SUB)
     total[place, :] = total[place, :] + part
 
+
+def grid_kernel(slot_cap, chunk, channels, feat, table, taper, out, total, left, right):
+    step = pl.program_id(0)
+
+    @pl.when(step == 0)
+    def _():
+        total[...] = jnp.zeros_like(total)
+
+    grid_chunk(
+        slot_cap, chunk, channels, step * LANES, feat[0], table, total, left, right
+    )
+
     @pl.when(step == pl.num_programs(0) - 1)
     def _():
         for b in range(BLK_DEV):
-            sub = total[pl.ds(b * SUB, SUB), :] * taper[...]
-            out[slot_of[b]] = sub.astype(jnp.bfloat16)
+            out[b] = (total[pl.ds(b * SUB, SUB), :] * taper[...]).astype(jnp.bfloat16)
+
+
+def move_grid_kernel(
+    slot_cap, channels, send, table, taper, out, moved, total, left, right, own_sem, to_sem, at_sem
+):
+    count, features, chunk = send.shape
+    v, t = lax.axis_index("vis"), lax.axis_index("tile")
+    barrier = pltpu.get_barrier_semaphore()
+    for k in range(1, count):
+        pl.semaphore_signal(barrier, inc=1, device_id=((v + k) % count, t), device_id_type=MESH)
+    pl.semaphore_wait(barrier, count - 1)
+
+    def copy(k):
+        return pltpu.make_async_remote_copy(
+            src_ref=send.at[(v + k) % count],
+            dst_ref=moved.at[v],
+            send_sem=to_sem.at[k],
+            recv_sem=at_sem.at[k],
+            device_id=((v + k) % count, t),
+            device_id_type=MESH,
+        )
+
+    own = pltpu.make_async_copy(send.at[v], moved.at[v], own_sem.at[0])
+    own.start()
+    for k in range(1, count):
+        copy(k).start()
+    total[...] = jnp.zeros_like(total)
+    own.wait()
+
+    def source(k, _):
+        @pl.when(k > 0)
+        def _():
+            copy(k).wait_recv()
+
+        origin = (v + count - k) % count
+
+        def part(piece, _):
+            lane = pl.multiple_of(piece * LANES, LANES)
+            grid_chunk(
+                slot_cap,
+                chunk,
+                channels,
+                lane,
+                moved[origin, :, pl.ds(lane, LANES)],
+                table,
+                total,
+                left,
+                right,
+            )
+            return 0
+
+        lax.fori_loop(0, chunk // LANES, part, 0)
+        return 0
+
+    lax.fori_loop(0, count, source, 0)
+    for b in range(BLK_DEV):
+        out[b] = (total[pl.ds(b * SUB, SUB), :] * taper[...]).astype(jnp.bfloat16)
+    for k in range(1, count):
+        copy(k).wait_send()
+
+
+def slot_kernel(slot_of, subs, out):
+    out[...] = jnp.zeros_like(out)
+    for b in range(BLK_DEV):
+        out[slot_of[b]] = subs[b]
 
 
 def gather_kernel(subs, meta, out, meta_out, own_sem, near_send, near_recv, far_send, far_recv):
@@ -291,43 +360,60 @@
         ],
         name="dispatch",
     )(vis_data, u_cell, v_cell, u_frac, v_frac, w_plane, block_route.reshape(1, rows))
-    moved = lax.all_to_all(send, "vis", split_axis=0, concat_axis=0, tiled=True)
-    if chunk % LANES:
-        moved = jnp.transpose(moved, (1, 0, 2)).reshape(1, features, vis_count * chunk)
-    per_source = moved.shape[2] // LANES
-    steps = moved.shape[0] * per_source
-    covered = min(BLK_DEV, LANES // slot_cap)
-
     table = jnp.pad(kernel_taps.astype(jnp.bfloat16).astype(jnp.float32).T, ((0, 8 - TAPS), (0, 0)))
     taper = jnp.repeat(taper_gain, POLC, axis=1)
+    covered = min(BLK_DEV, LANES // slot_cap)
+    vmem = pl.BlockSpec(memory_space=pltpu.VMEM)
+    work = [
+        pltpu.VMEM((BLK_DEV * SUB, SUB * POLC), jnp.float32),
+        pltpu.VMEM((covered * SUB, channels * LANES), jnp.bfloat16),
+        pltpu.VMEM((SUB * POLC, channels * LANES), jnp.bfloat16),
+    ]
+    gridded = jax.ShapeDtypeStruct((BLK_DEV, SUB, SUB * POLC), jnp.bfloat16)
+    if chunk % LANES == 0:
+        subs = pl.pallas_call(
+            functools.partial(move_grid_kernel, slot_cap, channels),
+            in_specs=[vmem, vmem, vmem],
+            out_specs=vmem,
+            out_shape=gridded,
+            scratch_shapes=[pltpu.VMEM(send.shape, jnp.bfloat16)]
+            + work
+            + [
+                pltpu.SemaphoreType.DMA((1,)),
+                pltpu.SemaphoreType.DMA((vis_count,)),
+                pltpu.SemaphoreType.DMA((vis_count,)),
+            ],
+            compiler_params=pltpu.CompilerParams(collective_id=1, has_side_effects=True),
+            name="move_grid",
+        )(send, table, taper)
+    else:
+        moved = lax.all_to_all(send, "vis", split_axis=0, concat_axis=0, tiled=True)
+        moved = jnp.transpose(moved, (1, 0, 2)).reshape(1, features, vis_count * chunk)
+        subs = pl.pallas_call(
+            functools.partial(grid_kernel, slot_cap, chunk, channels),
+            grid=(moved.shape[2] // LANES,),
+            in_specs=[
+                pl.BlockSpec((1, features, LANES), lambda s: (0, 0, s)),
+                pl.BlockSpec(table.shape, lambda s: (0, 0)),
+                pl.BlockSpec(taper.shape, lambda s: (0, 0)),
+            ],
+            out_specs=pl.BlockSpec(gridded.shape, lambda s: (0, 0, 0)),
+            out_shape=gridded,
+            scratch_shapes=work,
+            name="grid",
+        )(moved, table, taper)
     tile_ids = sub_tile[:, 0]
     slot_of = tile_ids * SCAP + ranks(tile_ids)
     subs = pl.pallas_call(
-        functools.partial(grid_kernel, slot_cap, chunk, channels),
-        grid_spec=pltpu.PrefetchScalarGridSpec(
-            num_scalar_prefetch=1,
-            grid=(steps,),
-            in_specs=[
-                pl.BlockSpec(
-                    (1, features, LANES), lambda s, *_: (s // per_source, 0, s % per_source)
-                ),
-                pl.BlockSpec(table.shape, lambda s, *_: (0, 0)),
-                pl.BlockSpec(taper.shape, lambda s, *_: (0, 0)),
-            ],
-            out_specs=pl.BlockSpec((slots, SUB, SUB * POLC), lambda s, *_: (0, 0, 0)),
-            scratch_shapes=[
-                pltpu.VMEM((BLK_DEV * SUB, SUB * POLC), jnp.float32),
-                pltpu.VMEM((covered * SUB, channels * LANES), jnp.bfloat16),
-                pltpu.VMEM((SUB * POLC, channels * LANES), jnp.bfloat16),
-            ],
-        ),
+        slot_kernel,
+        in_specs=[pl.BlockSpec(memory_space=pltpu.SMEM), vmem],
+        out_specs=vmem,
         out_shape=jax.ShapeDtypeStruct((slots, SUB, SUB * POLC), jnp.bfloat16),
-        name="grid",
-    )(slot_of, moved, table, taper)
+        name="slot",
+    )(slot_of, subs)
     meta = jnp.concatenate([tile_ids, sub_anchor[:, 0], sub_anchor[:, 1]])
     meta = jnp.pad(meta, (0, LANES - meta.shape[0])).reshape(1, LANES)
     hops = (vis_count - 1) * tile_width * 2
-    vmem = pl.BlockSpec(memory_space=pltpu.VMEM)
     subs, meta = pl.pallas_call(
         gather_kernel,
         in_specs=[vmem, vmem],

time: 102 us -> 96.3 us (0.944)
  waiting for transfers between devices: 17.4 us -> 0 us
  Pallas kernels: 70.3 us -> 86.4 us
  starting transfers between devices: 7.3 us -> 0 us
  other arithmetic: 1.53 us -> 4.29 us
    all_to_all x1 -> x0, waiting for transfers between devices: 17.4 us -> none  [on_device(): moved = lax.all_to_all(send, 'vis', split_axis=0, concat_axis=0, tiled=True)]
    pallas_call x1 -> x2, Pallas kernels: 22.5 us -> 33.6 us  [the longest x1 32 us: on_device(): pl.pallas_call(functools.partial(move_grid_kernel, slot_cap, channels), i...]
    all_to_all x1 -> x0, starting transfers between devices: 7.3 us -> none  [on_device(): moved = lax.all_to_all(send, 'vis', split_axis=0, concat_axis=0, tiled=True)]
    pallas_call x1, Pallas kernels: 35.3 us -> 40.6 us  [on_device(): pl.pallas_call(gather_kernel, in_specs=[vmem, vmem], out_specs=[vmem, vme...]
  transfers between devices with their start and end apart: 1 -> 0, of which waited for: 1 -> 0; matrix products, arithmetic and copies ran while one was open for 3% -> 0% of each run, Pallas kernels for 0% -> 0%
where the time goes in v3:
time: 96.3 us; the launch traced here: 95.8 us
  Pallas kernels  86.4 us (90%)
  local copies, waits for them, and re-layouts  5.03 us (5%)
  other arithmetic  4.29 us (4%)
    pallas_call x1, Pallas kernels, on_device(): pl.pallas_call(gather_kernel, in_specs=[vmem, vmem], out_specs=[vmem, vme...  40.6 us
    pallas_call x1, Pallas kernels, on_device(): pl.pallas_call(functools.partial(move_grid_kernel, slot_cap, channels), i...  32 us
    pallas_call x1, Pallas kernels, on_device(): pl.pallas_call(functools.partial(place_kernel, per_owner), grid_spec=pltp...  6.98 us
    pallas_call x1, Pallas kernels, on_device(): pl.pallas_call(functools.partial(dispatch_kernel, slot_cap), out_shape=ja...  5.29 us

profile of v3, /device:TPU:0, one launch (start us, length us, event | category | flops | bytes accessed | tf_op | source)
XLA Modules:
  0.0 95.8 jit_solution(9354508773100414200)
XLA Ops:
  0.0 0.9 convert_reduce_fusion.1
  0.9 1.2 %multiply_add_fusion.slot_of = s32[8]{0:T(128)} fusion(s32[8]{0:T(128)S(1)} %convert_reduce_fusion.1, s32[8,1]{0,1:T(1,128)} %param.20), kind=kLoop, calls=%fused_computation.21 | loop fusion | flops 16 | bytes 96 | tf_op jit(solution)/shard_map/add | solution.py:406
  2.2 0.8 slice_bitcast_fusion.3
  2.9 0.7 pad_add_fusion
  3.6 0.5 pad_bitcast_fusion.meta
  4.2 0.7 convert_bitcast_fusion
  4.9 0.6 pad_convert_fusion.table
  5.5 0.8 copy.20
  6.3 0.7 copy.21.taper
  7.0 5.3 %dispatch.1.send = bf16[8,192,256]{2,1,0:T(8,128)(2,1)} custom-call(bf16[1024,128]{1,0:T(8,128)(2,1)} %vis.1, s32[16,1024]{1,0:T(8,128)} %u_cell.1, s32[16,1024]{1,0:T(8,128)} %v_cell.1, s32[16,1024]{1,0:T(8,128)} %u_frac.1, s32[16,1024]{1,0:T(8,128)} %v_frac.1, s32[16,1024]{1,0:T(8,128)} %w_plane.1, s32[1,1024]{1,0:T(1,128)} %bitcast.35), custom_call_target="tpu_custom_call" | custom-call | tf_op jit(solution)/shard_map/dispatch/pallas_call | solution.py:354
  12.3 32.0 %move_grid.1.subs = bf16[8,32,256]{2,1,0:T(8,128)(2,1)} custom-call(bf16[8,192,256]{2,1,0:T(8,128)(2,1)} %dispatch.1.send, f32[8,128]{1,0:T(8,128)} %pad_convert_fusion.table, f32[32,256]{1,0:T(8,128)} %copy.21.taper), custom_call_target="tpu_custom_call" | custom-call | tf_op jit(solution)/shard_map/move_grid/pallas_call | solution.py:374
  44.2 1.6 %slot.1 = bf16[16,32,256]{2,1,0:T(8,128)(2,1)} custom-call(s32[8]{0:T(128)} %multiply_add_fusion.slot_of, bf16[8,32,256]{2,1,0:T(8,128)(2,1)} %move_grid.1.subs), custom_call_target="tpu_custom_call" | custom-call | tf_op jit(solution)/shard_map/slot/pallas_call | solution.py:407
  45.9 40.6 %gather.1 = (bf16[8,4,4,32,256]{4,3,2,1,0:T(8,128)(2,1)}, s32[8,4,1,128]{3,2,1,0:T(1,128)}) custom-call(bf16[4,4,32,256]{3,2,1,0:T(8,128)(2,1)} %bitcast.31, s32[1,128]{1,0:T(1,128)} %pad_bitcast_fusion.meta), custom_call_target="tpu_custom_call" | custom-call | tf_op jit(solution)/shard_map/gather/pallas_call | solution.py:417
  86.4 0.8 copy.25
  87.2 0.1 convert_reduce_fusion
  87.4 0.1 copy.23
  87.5 0.6 add.36.offset_v
  88.1 0.1 copy.24
  88.2 0.7 mul.31.offset_u
  88.8 7.0 %place.1 = f32[2,32,2048]{2,1,0:T(8,128)} custom-call(s32[128]{0:T(128)} %add.36.offset_v, s32[128]{0:T(128)} %mul.31.offset_u, bf16[8,16,32,256]{3,2,1,0:T(8,128)(2,1)} %bitcast.30), custom_call_target="tpu_custom_call" | custom-call | tf_op jit(solution)/shard_map/place/pallas_call | solution.py:448
  (6 shorter events, 0.1 us)

commit v4 on v3

--- a/solution.py
+++ b/solution.py
@@ -17,13 +17,14 @@
 SCAP = 2
 LANES = 128
 ROWS = 8
+GROUP = 4
 FAR = 1 << 20
 MESH = pl.DeviceIdType.MESH
 NT = (((1,), (1,)), ((), ()))
 
 
 def dispatch_kernel(
-    slot_cap, vis, u_cell, v_cell, u_frac, v_frac, w_plane, route, out, feat, dest
+    slot_cap, vis, u_cell, v_cell, u_frac, v_frac, w_plane, route, taps, gain, out, table, taper, feat, dest
 ):
     rows = vis.shape[0]
     columns = vis.shape[1]
@@ -51,6 +52,24 @@
     rank = jnp.sum(onehot * before, axis=0, keepdims=True).astype(jnp.int32)
     dest[...] = names * slot_cap + rank
 
+    turn = lax.broadcasted_iota(jnp.int32, (ROWS, TAPS), 0) == lax.broadcasted_iota(
+        jnp.int32, (ROWS, TAPS), 1
+    )
+    table[...] = lax.dot_general(
+        jnp.where(turn, 1.0, 0.0).astype(jnp.bfloat16),
+        taps[...].astype(jnp.bfloat16),
+        NT,
+        preferred_element_type=jnp.float32,
+    )
+    cells = lax.broadcasted_iota(jnp.int32, (SUB, SUB * POLC), 0)
+    repeat = cells == lax.broadcasted_iota(jnp.int32, (SUB, SUB * POLC), 1) // POLC
+    taper[...] = jnp.dot(
+        gain[...],
+        jnp.where(repeat, 1.0, 0.0),
+        precision=lax.Precision.HIGHEST,
+        preferred_element_type=jnp.float32,
+    )
+
     def send(owner, _):
         slots = lax.broadcasted_iota(jnp.int32, (chunk, rows), 0) + owner * chunk
         pick = jnp.where(slots == dest[...], 1.0, 0.0).astype(jnp.bfloat16)
@@ -62,12 +81,14 @@
     lax.fori_loop(0, owners, send, 0)
 
 
-def spread(cell, taps, offsets):
-    delta = offsets - cell
-    weight = jnp.zeros(delta.shape, jnp.float32)
-    for tap in range(TAPS):
-        weight = jnp.where(delta == tap, taps[tap : tap + 1, :], weight)
-    return weight
+def spread(cell, taps):
+    rows = lax.broadcasted_iota(jnp.int32, taps.shape, 0) - cell
+    parts = []
+    for start in range(0, SUB, ROWS):
+        delta = rows + start
+        weight = jnp.take_along_axis(taps, delta & (ROWS - 1), axis=0)
+        parts.append(jnp.where((delta >= 0) & (delta < ROWS), weight, 0.0))
+    return jnp.concatenate(parts, axis=0)
 
 
 def grid_chunk(slot_cap, chunk, channels, lane, feat, table, total, left, right):
@@ -76,10 +97,10 @@
     columns = channels * POLC
     lanes = lax.broadcasted_iota(jnp.int32, (SUB, LANES), 1)
     block = (lane + lanes) % chunk // slot_cap - first
-    offsets = lax.broadcasted_iota(jnp.int32, (SUB, LANES), 0)
     samples = feat[:columns, :].astype(jnp.float32)
     codes = feat[columns:, :].astype(jnp.float32).astype(jnp.int32)
     lookup = table[...]
+    part = jnp.zeros((covered * SUB, SUB * POLC), jnp.float32)
     for h in range(channels):
         sample = samples[h * POLC : (h + 1) * POLC, :]
         cell_u = codes[h : h + 1, :]
@@ -88,8 +109,8 @@
         row_v = codes[3 * channels + h : 3 * channels + h + 1, :]
         taps_u = jnp.take_along_axis(lookup, jnp.broadcast_to(row_u, (8, LANES)), axis=1)
         taps_v = jnp.take_along_axis(lookup, jnp.broadcast_to(row_v, (8, LANES)), axis=1)
-        weight_u = spread(cell_u, taps_u, offsets)
-        weight_v = spread(cell_v, taps_v, offsets)
+        weight_u = spread(cell_u, taps_u)
+        weight_v = spread(cell_v, taps_v)
         here = pl.ds(h * LANES, LANES)
         weighted = weight_u[:, None, :] * sample[None, :, :]
         right[:, here] = weighted.reshape(SUB * POLC, LANES).astype(jnp.bfloat16)
@@ -97,7 +118,11 @@
             left[pl.ds(b * SUB, SUB), here] = jnp.where(block == b, weight_v, 0.0).astype(
                 jnp.bfloat16
             )
-    part = lax.dot_general(left[...], right[...], NT, preferred_element_type=jnp.float32)
+        if (h + 1) % GROUP == 0:
+            group = pl.ds((h + 1 - GROUP) * LANES, GROUP * LANES)
+            part = part + lax.dot_general(
+                left[:, group], right[:, group], NT, preferred_element_type=jnp.float32
+            )
     place = pl.ds(pl.multiple_of(first * SUB, SUB), covered * SUB)
     total[place, :] = total[place, :] + part
 
@@ -178,10 +203,19 @@
         copy(k).wait_send()
 
 
-def slot_kernel(slot_of, subs, out):
+def slot_kernel(tiles, anchors, subs, out, meta):
+    slots = out.shape[0]
     out[...] = jnp.zeros_like(out)
+    lanes = lax.broadcasted_iota(jnp.int32, meta.shape, 1)
+    places = jnp.full(meta.shape, -FAR, jnp.int32)
     for b in range(BLK_DEV):
-        out[slot_of[b]] = subs[b]
+        slot = tiles[b, 0] * SCAP
+        for before in range(b):
+            slot = slot + jnp.where(tiles[before, 0] == tiles[b, 0], 1, 0)
+        out[slot] = subs[b]
+        places = jnp.where(lanes == slot, anchors[b, 0], places)
+        places = jnp.where(lanes == slots + slot, anchors[b, 1], places)
+    meta[...] = places
 
 
 def gather_kernel(subs, meta, out, meta_out, own_sem, near_send, near_recv, far_send, far_recv):
@@ -282,7 +316,8 @@
     lax.fori_loop(0, count - 1, sent, 0)
 
 
-def place_kernel(tile_slots, offset_v, offset_u, subs, out, canvas):
+def place_kernel(tile_slots, meta, subs, out, canvas):
+    v, t = lax.axis_index("vis"), lax.axis_index("tile")
     step = pl.program_id(0)
     slots = subs.shape[1]
     height = out.shape[1]
@@ -294,8 +329,10 @@
         canvas[...] = jnp.zeros_like(canvas)
 
     def add_one(slot, _):
-        low = offset_v[step * slots + slot]
-        column = offset_u[step * slots + slot]
+        source = step * (slots // tile_slots) + slot // tile_slots
+        lane = t * tile_slots + slot % tile_slots
+        low = meta[source, lane] - v * height + SUB
+        column = meta[source, slots + lane] * POLC
 
         @pl.when((low > 0) & (low < height + SUB))
         def _():
@@ -345,23 +382,29 @@
     height = TS // vis_count
     width = TS * POLC
 
-    order = jnp.arange(BLK_DEV, dtype=jnp.int32)
-
-    def ranks(tiles):
-        same = tiles[..., :, None] == tiles[..., None, :]
-        return jnp.sum((same & (order[None, :] < order[:, None])).astype(jnp.int32), axis=-1)
-
-    send = pl.pallas_call(
+    send, table, taper = pl.pallas_call(
         functools.partial(dispatch_kernel, slot_cap),
-        out_shape=jax.ShapeDtypeStruct((vis_count, features, chunk), jnp.bfloat16),
+        out_shape=[
+            jax.ShapeDtypeStruct((vis_count, features, chunk), jnp.bfloat16),
+            jax.ShapeDtypeStruct((ROWS, LANES), jnp.float32),
+            jax.ShapeDtypeStruct((SUB, SUB * POLC), jnp.float32),
+        ],
         scratch_shapes=[
             pltpu.VMEM((features, rows), jnp.bfloat16),
             pltpu.VMEM((1, rows), jnp.int32),
         ],
         name="dispatch",
-    )(vis_data, u_cell, v_cell, u_frac, v_frac, w_plane, block_route.reshape(1, rows))
-    table = jnp.pad(kernel_taps.astype(jnp.bfloat16).astype(jnp.float32).T, ((0, 8 - TAPS), (0, 0)))
-    taper = jnp.repeat(taper_gain, POLC, axis=1)
+    )(
+        vis_data,
+        u_cell,
+        v_cell,
+        u_frac,
+        v_frac,
+        w_plane,
+        block_route.reshape(1, rows),
+        kernel_taps,
+        taper_gain,
+    )
     covered = min(BLK_DEV, LANES // slot_cap)
     vmem = pl.BlockSpec(memory_space=pltpu.VMEM)
     work = [
@@ -402,17 +445,17 @@
             scratch_shapes=work,
             name="grid",
         )(moved, table, taper)
-    tile_ids = sub_tile[:, 0]
-    slot_of = tile_ids * SCAP + ranks(tile_ids)
-    subs = pl.pallas_call(
+    scalars = pl.BlockSpec(memory_space=pltpu.SMEM)
+    subs, meta = pl.pallas_call(
         slot_kernel,
-        in_specs=[pl.BlockSpec(memory_space=pltpu.SMEM), vmem],
-        out_specs=vmem,
-        out_shape=jax.ShapeDtypeStruct((slots, SUB, SUB * POLC), jnp.bfloat16),
+        in_specs=[scalars, scalars, vmem],
+        out_specs=[vmem, vmem],
+        out_shape=[
+            jax.ShapeDtypeStruct((slots, SUB, SUB * POLC), jnp.bfloat16),
+            jax.ShapeDtypeStruct((1, LANES), jnp.int32),
+        ],
         name="slot",
-    )(slot_of, subs)
-    meta = jnp.concatenate([tile_ids, sub_anchor[:, 0], sub_anchor[:, 1]])
-    meta = jnp.pad(meta, (0, LANES - meta.shape[0])).reshape(1, LANES)
+    )(sub_tile, sub_anchor, subs)
     hops = (vis_count - 1) * tile_width * 2
     subs, meta = pl.pallas_call(
         gather_kernel,
@@ -435,20 +478,11 @@
         name="gather",
     )(subs.reshape(tile_width, per_owner, SUB, SUB * POLC), meta)
     subs = subs.reshape(vis_count, slots, SUB, SUB * POLC)
-    meta = meta.reshape(vis_count * tile_width, LANES)[:, : 3 * BLK_DEV]
-    meta = meta.reshape(vis_count * tile_width, 3, BLK_DEV)
-
-    wanted = jnp.arange(per_owner, dtype=jnp.int32)
-    tiles_all = meta[:, 0]
-    slot_all = (tiles_all - lax.axis_index("tile") * gt_dev) * SCAP + ranks(tiles_all)
-    hit = slot_all[:, None, :] == wanted[None, :, None]
-    low = jnp.sum(jnp.where(hit, meta[:, 1][:, None] + FAR, 0), axis=-1) - FAR
-    offset_v = (low - lax.axis_index("vis") * height + SUB).reshape(-1)
-    offset_u = jnp.sum(jnp.where(hit, meta[:, 2][:, None], 0), axis=-1).reshape(-1) * POLC
+    meta = meta.reshape(vis_count * tile_width, LANES)
     return pl.pallas_call(
         functools.partial(place_kernel, per_owner),
         grid_spec=pltpu.PrefetchScalarGridSpec(
-            num_scalar_prefetch=2,
+            num_scalar_prefetch=1,
             grid=(vis_count,),
             in_specs=[pl.BlockSpec((1, slots, SUB, SUB * POLC), lambda s, *_: (s, 0, 0, 0))],
             out_specs=pl.BlockSpec((gt_dev, height, width), lambda s, *_: (0, 0, 0)),
@@ -458,7 +492,7 @@
         ),
         out_shape=jax.ShapeDtypeStruct((gt_dev, height, width), jnp.float32),
         name="place",
-    )(offset_v, offset_u, subs)
+    )(meta, subs)
 
 
 def solution(mesh):

time: 96.3 us -> 90.8 us (0.943)
  other arithmetic: 4.29 us -> 0 us
    unnamed x2 -> x3, local copies, waits for them, and re-layouts: 1.57 us -> 4.08 us
    reshape x3 -> x0, local copies, waits for them, and re-layouts: 1.25 us -> none  [the longest x2 0.7 us: on_device(): taper = jnp.repeat(taper_gain, POLC, axis=1)]
    add x2 -> x0, other arithmetic: 1.24 us -> none  [the longest x1 1.23 us: on_device(): slot_of = tile_ids * SCAP + ranks(tile_ids)]
    pallas_call x1, Pallas kernels: 32 us -> 30.8 us  [on_device(): pl.pallas_call(functools.partial(move_grid_kernel, slot_cap, channels), i...]
    reduce_sum x3 -> x0, other arithmetic: 1.02 us -> none  [the longest x2 1 us: ranks(): jnp.sum((same & (order[None, :] < order[:, None])).astype(jnp.int32), axi...]
where the time goes in v4:
time: 90.8 us; the launch traced here: 90 us
  Pallas kernels  85.9 us (95%)
  local copies, waits for them, and re-layouts  4.08 us (4%)
    pallas_call x1, Pallas kernels, on_device(): pl.pallas_call(gather_kernel, in_specs=[vmem, vmem], out_specs=[vmem, vme...  40.5 us
    pallas_call x1, Pallas kernels, on_device(): pl.pallas_call(functools.partial(move_grid_kernel, slot_cap, channels), i...  30.8 us
    pallas_call x1, Pallas kernels, on_device(): pl.pallas_call(functools.partial(place_kernel, per_owner), grid_spec=pltp...  7.48 us
    pallas_call x1, Pallas kernels, on_device(): pl.pallas_call(functools.partial(dispatch_kernel, slot_cap), out_shape=[j...  5.39 us
    unnamed x3, local copies, waits for them, and re-layouts  4.08 us

profile of v4, /device:TPU:0, one launch (start us, length us, event | category | flops | bytes accessed | tf_op | source)
XLA Modules:
  0.0 90.0 jit_solution(12659625035732153625)
XLA Ops:
  0.0 1.3 %copy.13.tiles = s32[8,1]{1,0:T(8,128)} copy(s32[8,1]{0,1:T(1,128)} %param.20) | data formatting | bytes 64 | tf_op args[9]
  1.3 1.3 %copy.14.anchors = s32[8,2]{1,0:T(8,128)} copy(s32[8,2]{0,1:T(2,128)} %param.21) | data formatting | bytes 128 | tf_op args[10]
  2.7 1.4 %copy.12.taps = f32[128,7]{1,0:T(8,128)} copy(f32[128,7]{0,1:T(8,128)} %param.18) | data formatting | bytes 7168 | tf_op args[7]
  4.1 5.4 %dispatch.1 = (bf16[8,192,256]{2,1,0:T(8,128)(2,1)}, f32[8,128]{1,0:T(8,128)}, f32[32,256]{1,0:T(8,128)}) custom-call(bf16[1024,128]{1,0:T(8,128)(2,1)} %vis.1, s32[16,1024]{1,0:T(8,128)} %u_cell.1, s32[16,1024]{1,0:T(8,128)} %v_cell.1, s32[16,1024]{1,0:T(8,128)} %u_frac.1, s32[16,1024]{1,0:T(8,128)} %v_frac.1, s32[16,1024]{1,0:T(8,128)} %w_plane.1, ...), custom_call_target="tpu_custom_call" | custom-call | tf_op jit(solution)/shard_map/dispatch/pallas_call | solution.py:385
  9.5 30.8 %move_grid.1.subs = bf16[8,32,256]{2,1,0:T(8,128)(2,1)} custom-call(bf16[8,192,256]{2,1,0:T(8,128)(2,1)} %get-tuple-element.12.send, f32[8,128]{1,0:T(8,128)} %get-tuple-element.13.table, f32[32,256]{1,0:T(8,128)} %get-tuple-element.14.taper), custom_call_target="tpu_custom_call" | custom-call | tf_op jit(solution)/shard_map/move_grid/pallas_call | solution.py:417
  40.3 1.7 %slot.1 = (bf16[16,32,256]{2,1,0:T(8,128)(2,1)}, s32[1,128]{1,0:T(1,128)}) custom-call(s32[8,1]{1,0:T(8,128)} %copy.13.tiles, s32[8,2]{1,0:T(8,128)} %copy.14.anchors, bf16[8,32,256]{2,1,0:T(8,128)(2,1)} %move_grid.1.subs), custom_call_target="tpu_custom_call" | custom-call | tf_op jit(solution)/shard_map/slot/pallas_call | solution.py:449
  42.0 40.5 %gather.1 = (bf16[8,4,4,32,256]{4,3,2,1,0:T(8,128)(2,1)}, s32[8,4,1,128]{3,2,1,0:T(1,128)}) custom-call(bf16[4,4,32,256]{3,2,1,0:T(8,128)(2,1)} %bitcast.5, s32[1,128]{1,0:T(1,128)} %get-tuple-element.16.meta), custom_call_target="tpu_custom_call" | custom-call | tf_op jit(solution)/shard_map/gather/pallas_call | solution.py:460
  82.5 7.5 %place.1 = f32[2,32,2048]{2,1,0:T(8,128)} custom-call(s32[32,128]{1,0:T(8,128)} %bitcast.6, bf16[8,16,32,256]{3,2,1,0:T(8,128)(2,1)} %bitcast.4), custom_call_target="tpu_custom_call" | custom-call | tf_op jit(solution)/shard_map/place/pallas_call | solution.py:482

commit v5 on v4

--- a/solution.py
+++ b/solution.py
@@ -261,21 +261,27 @@
         ]
 
     def far(k, step):
-        side = 1 - 2 * (k % 2)
-        origin = member(spot - side * step)
         source = (t + width - k) % width
-        refs = (out.at[origin, pl.ds(source, 1)], meta_out.at[origin, source])
-        return [
-            pltpu.make_async_remote_copy(
-                src_ref=ref,
-                dst_ref=ref,
-                send_sem=far_send.at[(step * width + k) * 2 + i],
-                recv_sem=far_recv.at[(step * width + k) * 2 + i],
-                device_id=(member(spot + side), t),
-                device_id_type=MESH,
+        cut = out.shape[2] // 2
+        copies = []
+        for i in range(3):
+            side = 1 - 2 * (i % 2)
+            origin = member(spot - side * step)
+            if i < 2:
+                ref = out.at[origin, source, pl.ds(i * cut, cut)]
+            else:
+                ref = meta_out.at[origin, source]
+            copies.append(
+                pltpu.make_async_remote_copy(
+                    src_ref=ref,
+                    dst_ref=ref,
+                    send_sem=far_send.at[(step * width + k) * 3 + i],
+                    recv_sem=far_recv.at[(step * width + k) * 3 + i],
+                    device_id=(member(spot + side), t),
+                    device_id_type=MESH,
+                )
             )
-            for i, ref in enumerate(refs)
-        ]
+        return copies
 
     for copy in own():
         copy.start()
@@ -293,9 +299,8 @@
 
     def forward(step, _):
         for k in range(width):
-            for copy in far(k, step - 1):
-                copy.wait_recv()
-            for copy in far(k, step):
+            for landed, copy in zip(far(k, step - 1), far(k, step)):
+                landed.wait_recv()
                 copy.start()
         return 0
 
@@ -328,28 +333,28 @@
     def _():
         canvas[...] = jnp.zeros_like(canvas)
 
-    def add_one(slot, _):
-        source = step * (slots // tile_slots) + slot // tile_slots
-        lane = t * tile_slots + slot % tile_slots
-        low = meta[source, lane] - v * height + SUB
-        column = meta[source, slots + lane] * POLC
-
-        @pl.when((low > 0) & (low < height + SUB))
-        def _():
-            sub = subs[0, slot].astype(jnp.float32)
-            sub = jnp.concatenate([sub, jnp.zeros((SUB, LANES), jnp.float32)], axis=1)
-            sub = pltpu.roll(sub, column % LANES, 1)
-            sub = jnp.concatenate([sub, jnp.zeros((ROWS, span + LANES), jnp.float32)], axis=0)
-            sub = pltpu.roll(sub, low % ROWS, 0)
-            top = pl.multiple_of(low // ROWS * ROWS, ROWS)
-            base = pl.multiple_of(column // LANES * LANES, LANES)
-            tile = slot % tile_slots // SCAP
-            here = (tile, pl.ds(top, SUB + ROWS), pl.ds(base, span + LANES))
-            canvas[here] = canvas[here] + sub
+    def add_source(near, _):
+        source = step * (slots // tile_slots) + near
+        for slot in range(tile_slots):
+            lane = t * tile_slots + slot
+            low = meta[source, lane] - v * height + SUB
+            column = meta[source, slots + lane] * POLC
+
+            @pl.when((low > 0) & (low < height + SUB))
+            def _():
+                sub = subs[0, near * tile_slots + slot].astype(jnp.float32)
+                sub = jnp.concatenate([sub, jnp.zeros((SUB, LANES), jnp.float32)], axis=1)
+                sub = pltpu.roll(sub, column % LANES, 1)
+                sub = jnp.concatenate([sub, jnp.zeros((ROWS, span + LANES), jnp.float32)], axis=0)
+                sub = pltpu.roll(sub, low % ROWS, 0)
+                top = pl.multiple_of(low // ROWS * ROWS, ROWS)
+                base = pl.multiple_of(column // LANES * LANES, LANES)
+                here = (slot // SCAP, pl.ds(top, SUB + ROWS), pl.ds(base, span + LANES))
+                canvas[here] = canvas[here] + sub
 
         return 0
 
-    lax.fori_loop(0, slots, add_one, 0)
+    lax.fori_loop(0, slots // tile_slots, add_source, 0)
 
     @pl.when(step == pl.num_programs(0) - 1)
     def _():
@@ -456,7 +461,7 @@
         ],
         name="slot",
     )(sub_tile, sub_anchor, subs)
-    hops = (vis_count - 1) * tile_width * 2
+    hops = (vis_count - 1) * tile_width * 3
     subs, meta = pl.pallas_call(
         gather_kernel,
         in_specs=[vmem, vmem],

time: 90.8 us -> 86.6 us (0.954)
  Pallas kernels: 85.9 us -> 82 us
    pallas_call x1, Pallas kernels: 40.5 us -> 37.3 us  [on_device(): pl.pallas_call(gather_kernel, in_specs=[vmem, vmem], out_specs=[vmem, vme...]
where the time goes in v5:
time: 86.6 us; the launch traced here: 86.1 us
  Pallas kernels  82 us (95%)
  local copies, waits for them, and re-layouts  4.08 us (5%)
    pallas_call x1, Pallas kernels, on_device(): pl.pallas_call(gather_kernel, in_specs=[vmem, vmem], out_specs=[vmem, vme...  37.3 us
    pallas_call x1, Pallas kernels, on_device(): pl.pallas_call(functools.partial(move_grid_kernel, slot_cap, channels), i...  30.8 us
    pallas_call x1, Pallas kernels, on_device(): pl.pallas_call(functools.partial(place_kernel, per_owner), grid_spec=pltp...  6.85 us
    pallas_call x1, Pallas kernels, on_device(): pl.pallas_call(functools.partial(dispatch_kernel, slot_cap), out_shape=[j...  5.39 us
    unnamed x3, local copies, waits for them, and re-layouts  4.08 us

profile of v5, /device:TPU:0, one launch (start us, length us, event | category | flops | bytes accessed | tf_op | source)
XLA Modules:
  0.0 86.1 jit_solution(11509528332498843123)
XLA Ops:
  0.0 1.3 %copy.13.tiles = s32[8,1]{1,0:T(8,128)} copy(s32[8,1]{0,1:T(1,128)} %param.20) | data formatting | bytes 64 | tf_op args[9]
  1.3 1.3 %copy.14.anchors = s32[8,2]{1,0:T(8,128)} copy(s32[8,2]{0,1:T(2,128)} %param.21) | data formatting | bytes 128 | tf_op args[10]
  2.7 1.4 %copy.12.taps = f32[128,7]{1,0:T(8,128)} copy(f32[128,7]{0,1:T(8,128)} %param.18) | data formatting | bytes 7168 | tf_op args[7]
  4.1 5.4 %dispatch.1 = (bf16[8,192,256]{2,1,0:T(8,128)(2,1)}, f32[8,128]{1,0:T(8,128)}, f32[32,256]{1,0:T(8,128)}) custom-call(bf16[1024,128]{1,0:T(8,128)(2,1)} %vis.1, s32[16,1024]{1,0:T(8,128)} %u_cell.1, s32[16,1024]{1,0:T(8,128)} %v_cell.1, s32[16,1024]{1,0:T(8,128)} %u_frac.1, s32[16,1024]{1,0:T(8,128)} %v_frac.1, s32[16,1024]{1,0:T(8,128)} %w_plane.1, ...), custom_call_target="tpu_custom_call" | custom-call | tf_op jit(solution)/shard_map/dispatch/pallas_call | solution.py:390
  9.5 30.8 %move_grid.1.subs = bf16[8,32,256]{2,1,0:T(8,128)(2,1)} custom-call(bf16[8,192,256]{2,1,0:T(8,128)(2,1)} %get-tuple-element.12.send, f32[8,128]{1,0:T(8,128)} %get-tuple-element.13.table, f32[32,256]{1,0:T(8,128)} %get-tuple-element.14.taper), custom_call_target="tpu_custom_call" | custom-call | tf_op jit(solution)/shard_map/move_grid/pallas_call | solution.py:422
  40.3 1.7 %slot.1 = (bf16[16,32,256]{2,1,0:T(8,128)(2,1)}, s32[1,128]{1,0:T(1,128)}) custom-call(s32[8,1]{1,0:T(8,128)} %copy.13.tiles, s32[8,2]{1,0:T(8,128)} %copy.14.anchors, bf16[8,32,256]{2,1,0:T(8,128)(2,1)} %move_grid.1.subs), custom_call_target="tpu_custom_call" | custom-call | tf_op jit(solution)/shard_map/slot/pallas_call | solution.py:454
  42.0 37.3 %gather.1 = (bf16[8,4,4,32,256]{4,3,2,1,0:T(8,128)(2,1)}, s32[8,4,1,128]{3,2,1,0:T(1,128)}) custom-call(bf16[4,4,32,256]{3,2,1,0:T(8,128)(2,1)} %bitcast.5, s32[1,128]{1,0:T(1,128)} %get-tuple-element.16.meta), custom_call_target="tpu_custom_call" | custom-call | tf_op jit(solution)/shard_map/gather/pallas_call | solution.py:465
  79.3 6.8 %place.1 = f32[2,32,2048]{2,1,0:T(8,128)} custom-call(s32[32,128]{1,0:T(8,128)} %bitcast.6, bf16[8,16,32,256]{3,2,1,0:T(8,128)(2,1)} %bitcast.4), custom_call_target="tpu_custom_call" | custom-call | tf_op jit(solution)/shard_map/place/pallas_call | solution.py:487
